TPU v7x, 128 devices: a whole 4x4x4 slice. The times are simulated.
128 devices in a mesh: gx: 16 (over x, z), gy: 8 (over y, core).
Axes of the slice: x: 4, y: 4, z: 4, core: 2. Of those that a mesh axis runs over, the one named last changes fastest.
Arguments:
- features: bfloat16 [256, 512, 512], P('gx', 'gy'), may hold values from -6 to 6
- cotangent: bfloat16 [256, 512, 512], P('gx', 'gy'), may hold values from -6 to 6
- low: int32 [256, 512], P('gx', 'gy'), may hold values from 0 to 7, as said below
- high: int32 [256, 512], P('gx', 'gy'), may hold values from 0 to 8, as said below
- weight_one: bfloat16 [27, 64, 64], replicated, may hold values from -0.4375 to 0.4375
- weight_two: bfloat16 [27, 64, 64], replicated, may hold values from -0.4375 to 0.4375
- scale_one: float32 [64], replicated, may hold values from 0.5 to 2
- shift_one: float32 [64], replicated, may hold values from -1.5 to 1.5
- scale_two: float32 [64], replicated, may hold values from 0.5 to 2
- shift_two: float32 [64], replicated, may hold values from -1.5 to 1.5
Outputs:
- output: bfloat16 [256, 512, 512], P('gx', 'gy')
- grad_features: bfloat16 [256, 512, 512], P('gx', 'gy')
- grad_weight_one: float32 [27, 64, 64], replicated
- grad_weight_two: float32 [27, 64, 64], replicated
Inputs may be any that keep to these rules, and one draw needn't show every extreme that they name: An empty column has low = high = 0; an occupied one has low < high. One device holds at most 4 filled bricks and some device holds exactly that many; the devices that share a gy index hold at most 2 filled bricks a device together, and some such group holds exactly that many. `high`: see low.
All inputs are finite; a program needn't handle non-finite values.
Results may differ from a plain program's by a relative error of at most 0.0071.
Values may be sent and summed in bfloat16 or wider, within the bound.
A program may use at most 256 MiB of HBM per device.

v0:
```python
import functools

import jax
import jax.numpy as jnp
from jax import lax
from jax.sharding import Mesh
from jax.sharding import PartitionSpec as P

BRICK = 8
ACT_MAX = 4
SHARE = 2
GY = ("gy_0", "gy_1")
GX = ("gx_0", "gx_1")
GX_GY = ("gx_0", "gx_1", "gy_0", "gy_1")


def from_behind(array, axis, by):
    devices = lax.axis_size(axis)
    pairs = [(i, i + by) for i in range(devices) if 0 <= i + by < devices]
    return lax.ppermute(array, axis, pairs)


def extended(array, sides, width):
    for axis, dim in sides:
        devices, length = (lax.axis_size(axis), array.shape[dim])
        up = [(i, (i + 1) % devices) for i in range(devices - 1)]
        down = [(j, i) for i, j in up]
        last = lax.slice_in_dim(array, length - width, length, axis=dim)
        initial = lax.slice_in_dim(array, 0, width, axis=dim)
        before = lax.ppermute(last, axis, up)
        after = lax.ppermute(initial, axis, down)
        array = jnp.concatenate([before, array, after], axis=dim)
    return array


def over_axes(array, axes):
    return functools.reduce(lax.psum, axes, array)


def spread_depth(column_mask, channels):
    return jnp.repeat(column_mask, channels, axis=-1)


def flat_dot(window, banded):
    flat_rows = window.reshape(-1, window.shape[-1])
    product = jnp.dot(flat_rows, banded, preferred_element_type=jnp.float32)
    return product.reshape(window.shape[:-1] + (banded.shape[1],))


def make_banded(weight, layers):
    channels = weight.shape[1]
    kernel = weight.reshape(9, 3, channels, channels).astype(jnp.float32)
    levels = jnp.arange(layers)
    banded = jnp.zeros((9, layers, channels, layers, channels), jnp.float32)
    for lift_index in range(3):
        stepper = (levels[:, None] - levels[None, :] == lift_index - 1).astype(jnp.float32)
        banded = banded + jnp.einsum("ab,jco->jacbo", stepper, kernel[:, lift_index])
    return banded.reshape(9, layers * channels, layers * channels).astype(jnp.bfloat16)


def forward_conv(source, banded):
    extent = source.shape[1] - 2
    running = jnp.zeros((source.shape[0], extent, extent, banded.shape[2]), jnp.float32)
    for offset in range(9):
        shift_x, shift_y = (offset // 3, offset % 3)
        window = source[:, shift_x : shift_x + extent, shift_y : shift_y + extent, :]
        running = running + flat_dot(window, banded[offset])
    return running


def adjoint_conv(errors, banded):
    extent = errors.shape[1] + 2
    width = errors.shape[-1]
    padded = jnp.pad(errors, ((0, 0), (2, 2), (2, 2), (0, 0)))
    running = jnp.zeros((errors.shape[0], extent, extent, width), jnp.float32)
    for offset in range(9):
        shift_x, shift_y = (2 - offset // 3, 2 - offset % 3)
        window = padded[:, shift_x : shift_x + extent, shift_y : shift_y + extent, :]
        product = lax.dot_general(
            window.reshape(-1, width),
            banded[offset],
            (((1,), (1,)), ((), ())),
            preferred_element_type=jnp.float32,
        )
        running = running + product.reshape(running.shape)
    return running


def weight_grad(source, errors):
    extent = errors.shape[1]
    flat_errors = errors.reshape(-1, errors.shape[-1])
    products = []
    for offset in range(9):
        shift_x, shift_y = (offset // 3, offset % 3)
        window = source[:, shift_x : shift_x + extent, shift_y : shift_y + extent, :].reshape(
            -1, source.shape[-1]
        )
        products.append(
            lax.dot_general(
                window, flat_errors, (((0,), (0,)), ((), ())), preferred_element_type=jnp.float32
            )
        )
    return jnp.stack(products)


def fold_banded(sums, channels):
    layers = sums.shape[1] // channels
    blocks = sums.reshape(9, layers, channels, layers, channels)
    lifted = [
        jnp.sum(jnp.diagonal(blocks, offset=1 - lift_index, axis1=1, axis2=3), axis=-1)
        for lift_index in range(3)
    ]
    return jnp.stack(lifted, axis=1).reshape(27, channels, channels)


def silu_slope(values):
    logistic = jax.nn.sigmoid(values)
    return logistic * (1.0 + values * (1.0 - logistic))


def brick_work(
    regions, occupied, targets, banded_one, banded_two, scale_one, shift_one, scale_two, shift_two
):
    channels = regions.shape[-1] // occupied.shape[-1]
    margin_mask = spread_depth(occupied, channels).astype(jnp.float32)
    interior = margin_mask[:, 1:-1, 1:-1]
    pre_one = forward_conv(regions, banded_one) * scale_one + shift_one
    hidden = (jax.nn.silu(pre_one) * margin_mask).astype(jnp.bfloat16)
    centre = regions[:, 2:-2, 2:-2].astype(jnp.float32)
    pre_two = forward_conv(hidden, banded_two) * scale_two + shift_two + centre
    result = (jax.nn.silu(pre_two) * interior).astype(jnp.bfloat16)
    grad_two = targets.astype(jnp.float32) * interior * silu_slope(pre_two)
    error_two = (grad_two * scale_two).astype(jnp.bfloat16)
    weight_sum_two = weight_grad(hidden, error_two)
    grad_one = adjoint_conv(error_two, banded_two) * margin_mask * silu_slope(pre_one)
    error_one = (grad_one * scale_one).astype(jnp.bfloat16)
    weight_sum_one = weight_grad(regions, error_one)
    grad_input = adjoint_conv(error_one, banded_one) + jnp.pad(
        grad_two, ((0, 0), (2, 2), (2, 2), (0, 0))
    )
    return (result, grad_input, weight_sum_one, weight_sum_two)


def cut_regions(field_pad, mask_pad, cotangent, brick_slots, bricks_y):
    zero_index = jnp.zeros((), jnp.int32)

    def single_brick(slot_id):
        corner_x = slot_id // bricks_y * BRICK
        corner_y = slot_id % bricks_y * BRICK
        region = lax.dynamic_slice(
            field_pad, (corner_x, corner_y, zero_index), (BRICK + 4, BRICK + 4, field_pad.shape[2])
        )
        occupied = lax.dynamic_slice(
            mask_pad,
            (corner_x + 1, corner_y + 1, zero_index),
            (BRICK + 2, BRICK + 2, mask_pad.shape[2]),
        )
        target = lax.dynamic_slice(
            cotangent, (corner_x, corner_y, zero_index), (BRICK, BRICK, cotangent.shape[2])
        )
        return (region, occupied, target)

    return jax.vmap(single_brick)(brick_slots)


def pass_rows(border, shift_by):
    return from_behind(border.astype(jnp.bfloat16), GY, shift_by).astype(border.dtype)


def pass_columns(border, shift_by):
    return from_behind(border.astype(jnp.bfloat16), GX, shift_by).astype(border.dtype)


def shards(
    features,
    cotangent,
    low,
    high,
    weight_one,
    weight_two,
    scale_one,
    shift_one,
    scale_two,
    shift_two,
):
    channels = weight_one.shape[1]
    layers = BRICK
    width = features.shape[2]
    heights = jnp.arange(layers, dtype=jnp.int32)
    column_mask = ((heights >= low[..., None]) & (heights < high[..., None])).astype(jnp.bfloat16)
    masked_features = features * spread_depth(column_mask, channels)
    field_pad, mask_pad = (
        extended(masked_features, ((GX, 0), (GY, 1)), 2),
        extended(column_mask, ((GX, 0), (GY, 1)), 2),
    )
    bricks_x = features.shape[0] // layers
    bricks_y = features.shape[1] // layers
    filled = (
        (high > low)
        .reshape(bricks_x, layers, bricks_y, layers)
        .any(axis=(1, 3))
        .reshape(-1)
        .astype(jnp.int32)
    )
    own_count = jnp.sum(filled)
    ranked = jnp.cumsum(filled) - 1
    listing = jnp.arange(ACT_MAX, dtype=jnp.int32)
    picked = (filled[None, :] == 1) & (ranked[None, :] == listing[:, None])
    brick_slots = jnp.sum(picked * jnp.arange(filled.shape[0], dtype=jnp.int32)[None, :], axis=1)
    live_rows = (listing < own_count).astype(jnp.bfloat16)[:, None, None, None]
    regions, occupied, targets = cut_regions(field_pad, mask_pad, cotangent, brick_slots, bricks_y)
    regions = regions * live_rows
    occupied = occupied * live_rows
    targets = targets * live_rows
    banded_one = make_banded(weight_one, layers)
    banded_two = make_banded(weight_two, layers)
    tiled = (
        jnp.tile(scale_one, layers),
        jnp.tile(shift_one, layers),
        jnp.tile(scale_two, layers),
        jnp.tile(shift_two, layers),
    )
    results, grad_regions, weight_sum_one, weight_sum_two = brick_work(
        regions, occupied, targets, banded_one, banded_two, tiled[0], tiled[1], tiled[2], tiled[3]
    )
    zero_index = jnp.zeros((), jnp.int32)

    def deposit(position, carried_grids):
        out_grid, grad_grid = carried_grids
        slot_id = brick_slots[position]
        corner_x = slot_id // bricks_y * layers
        corner_y = slot_id % bricks_y * layers
        corner = (corner_x, corner_y, zero_index)
        current = lax.dynamic_slice(out_grid, corner, (layers, layers, width))
        out_grid = lax.dynamic_update_slice(out_grid, current + results[position], corner)
        current_grad = lax.dynamic_slice(grad_grid, corner, (layers + 4, layers + 4, width))
        grad_grid = lax.dynamic_update_slice(
            grad_grid, current_grad + grad_regions[position], corner
        )
        return (out_grid, grad_grid)

    initial = (
        jnp.zeros(features.shape, jnp.bfloat16),
        jnp.zeros((features.shape[0] + 4, features.shape[1] + 4, width), jnp.float32),
    )
    out_grid, grad_grid = lax.fori_loop(0, ACT_MAX, deposit, initial)
    middle = grad_grid[:, 2:-2]
    middle = middle.at[:, -2:].add(pass_rows(grad_grid[:, :2], -1))
    middle = middle.at[:, :2].add(pass_rows(grad_grid[:, -2:], 1))
    interior = middle[2:-2]
    interior = interior.at[-2:].add(pass_columns(middle[:2], -1))
    interior = interior.at[:2].add(pass_columns(middle[-2:], 1))
    grad_features = (interior * spread_depth(column_mask, channels).astype(jnp.float32)).astype(
        jnp.bfloat16
    )
    folded_one = fold_banded(weight_sum_one, channels)
    folded_two = fold_banded(weight_sum_two, channels)
    summed = (over_axes(folded_one, GX_GY), over_axes(folded_two, GX_GY))
    capacity = lax.axis_size(GX) * lax.axis_size(GY) * SHARE
    return (out_grid, grad_features, summed[0] / capacity, summed[1] / capacity)


def solution(mesh):
    torus = Mesh(mesh.devices.reshape(4, 4, 4, 2), ("gx_0", "gx_1", "gy_0", "gy_1"))
    placed = (P(GX, GY, None), P(GX, GY, None), P(GX, GY), P(GX, GY), P(), P(), P(), P(), P(), P())
    return jax.shard_map(
        shards,
        mesh=torus,
        in_specs=placed,
        out_specs=(P(GX, GY, None), P(GX, GY, None), P(), P()),
        check_vma=False,
    )
```

profile of v0, /device:TPU:1, one launch (start us, length us, event | category | flops | bytes accessed | tf_op | source)
XLA Modules:
  0.0 576.6 jit_solution(1513502519343762787)
XLA Ops:
  9.3 5.0 collective-permute-start.4
  16.7 3.3 reshape.660
  22.3 4.2 collective-permute-start
  32.8 13.9 %while.27 = (s32[]{:T(128)}, bf16[16,64,512]{2,1,0:T(8,128)(2,1)}, s32[4,3]{1,0:T(4,128)S(1)}, bf16[4,8,8,512]{3,2,1,0:T(8,128)(2,1)}, s32[]{:T(128)}) while((s32[]{:T(128)}, bf16[16,64,512]{2,1,0:T(8,128)(2,1)}, s32[4,3]{1,0:T(4,128)S(1)}, bf16[4,8,8,512]{3,2,1,0:T(8,128)(2,1)}, s32[]{:T(128)}) %tuple.163), condition=%wide.while_cond.6, body=%wide.while_body.6.sunk | while | flops 2 | bytes 132213 | solution.py:158
  33.5 2.8 bitcast_dynamic-update-slice_fusion.8
  37.0 2.8 bitcast_dynamic-update-slice_fusion.8
  40.4 2.9 bitcast_dynamic-update-slice_fusion.8
  43.9 2.9 bitcast_dynamic-update-slice_fusion.8
  46.7 10.2 %fusion.1 = (bf16[9,8,64,8,64]{4,3,2,1,0:T(8,128)(2,1)S(1)}, bf16[9,8,64,8,64]{4,3,2,1,0:T(8,128)(2,1)}) fusion(f32[9,64,64]{2,1,0:T(8,128)S(1)} %get-tuple-element.356, f32[8,8]{1,0:T(8,128)S(1)} %fusion.111, f32[9,64,64]{2,1,0:T(8,128)S(1)} %get-tuple-element.357, f32[8,8]{1,0:T(8,128)S(1)} %fusion.110, f32[9,64,64]{2,1,0:T(8,128)S(1)} %get-tuple-element.355, ...), kind=kLoop, calls=%fused_computation.17 | loop fusion | flops 28311552 | bytes 10322688 | tf_op jit(solution)/shard_map/convert_element_type | solution.py:58
  57.0 8.2 %fusion.137 = (bf16[1,8,64,8,64]{4,3,2,1,0:T(8,128)(2,1)S(1)}, bf16[1,8,64,8,64]{4,3,2,1,0:T(8,128)(2,1)}, bf16[1,8,64,8,64]{4,3,2,1,0:T(8,128)(2,1)}, bf16[1,8,...) fusion(bf16[9,8,64,8,64]{4,3,2,1,0:T(8,128)(2,1)} %get-tuple-el, ...), kind=kLoop, calls=%fused_computation.296 | loop fusion | bytes 18874368 | tf_op jit(solution)/shard_map/slice | solution.py:67
  69.7 2.6 reshape.796
  72.2 2.6 reshape.797
  74.8 2.5 reshape.798
  77.3 2.6 reshape.799
  79.9 2.6 reshape.800
  82.5 2.6 reshape.801
  95.6 2.7 reshape.806
  98.4 3.2 collective-permute-start.7
  101.7 3.2 collective-permute-start.6
  110.0 2.6 reshape.809
  112.5 2.6 reshape.810
  115.1 2.6 reshape.811
  119.2 10.2 %while.26 = (s32[]{:T(128)}, bf16[20,68,8]{1,2,0:T(8,128)(2,1)S(1)}, s32[4,3]{1,0:T(4,128)}, bf16[4,10,10,8]{2,3,1,0:T(8,128)(2,1)S(1)}, s32[]{:T(128)}) while((s32[]{:T(128)}, bf16[20,68,8]{1,2,0:T(8,128)(2,1)S(1)}, s32[4,3]{1,0:T(4,128)}, bf16[4,10,10,8]{2,3,1,0:T(8,128)(2,1)S(1)}, s32[]{:T(128)}) %tuple.181), condition=%wide.while_cond.5, body=%wide.while_body.5.sunk | while | flops 2 | bytes 41085 | solution.py:153
  132.1 3.6 collective-permute-start.2
  139.8 13.7 %while.25 = (s32[]{:T(128)}, bf16[20,68,512]{2,1,0:T(8,128)(2,1)S(1)}, s32[4,3]{1,0:T(4,128)}, bf16[4,12,12,512]{3,2,1,0:T(8,128)(2,1)}, s32[]{:T(128)}) while((s32[]{:T(128)}, bf16[20,68,512]{2,1,0:T(8,128)(2,1)S(1)}, s32[4,3]{1,0:T(4,128)}, bf16[4,12,12,512]{3,2,1,0:T(8,128)(2,1)}, s32[]{:T(128)}) %tuple.160), condition=%wide.while_cond.4, body=%wide.while_body.4.sunk | while | flops 2 | bytes 345205 | solution.py:150
  213.3 2.7 stack.84
  216.0 3.3 copy_dynamic-update-slice_fusion.17
  219.4 2.7 stack.85
  222.1 2.7 stack.86
  224.7 2.8 stack.87
  227.6 2.7 stack.88
  230.3 2.8 stack.89
  233.1 2.7 stack.90
  235.8 2.9 stack.91
  240.5 3.5 copy_dynamic-update-slice_fusion.16
  258.8 7.1 %gather_fusion.3 = f32[7,9,64,64]{3,2,1,0:T(8,128)S(1)} fusion(f32[9,64,64,8,8]{2,1,4,3,0:T(8,128)} %bitcast.362, s32[7]{0:T(128)S(1)} %copy-done.49), kind=kCustom, calls=%fused_computation.1.clone | custom fusion | bytes 2064440 | tf_op jit(solution)/shard_map/jit(diagonal)/gather | solution.py:110
  265.9 8.4 %gather_fusion = f32[8,9,64,64]{3,2,1,0:T(8,128)} fusion(f32[9,64,64,8,8]{2,1,4,3,0:T(8,128)} %bitcast.363, s32[8]{0:T(128)S(1)} %copy-done.50), kind=kCustom, calls=%fused_computation.4 | custom fusion | bytes 2359360 | tf_op jit(solution)/shard_map/jit(diagonal)/gather | solution.py:110
  274.3 2.7 stack.98
  277.1 3.3 copy_dynamic-update-slice_fusion.8
  280.3 2.7 stack.99
  283.0 2.7 stack.100
  285.7 2.7 stack.101
  288.4 2.7 stack.102
  291.1 2.7 stack.103
  293.8 2.8 stack.104
  296.6 2.7 stack.105
  299.2 3.0 stack.106
  302.2 3.5 copy_dynamic-update-slice_fusion.7
  320.5 8.3 %gather_fusion.5 = f32[7,9,64,64]{3,2,1,0:T(8,128)} fusion(f32[9,64,64,8,8]{2,1,4,3,0:T(8,128)} %bitcast.365, s32[7]{0:T(128)S(1)} %copy-done.49), kind=kCustom, calls=%fused_computation.3.clone | custom fusion | bytes 2064440 | tf_op jit(solution)/shard_map/jit(diagonal)/gather | solution.py:110
  328.8 8.5 %gather_fusion.1 = f32[8,9,64,64]{3,2,1,0:T(8,128)} fusion(f32[9,64,64,8,8]{2,1,4,3,0:T(8,128)} %bitcast.366, s32[8]{0:T(128)S(1)} %copy-done.50), kind=kCustom, calls=%fused_computation.5 | custom fusion | bytes 2359360 | tf_op jit(solution)/shard_map/jit(diagonal)/gather | solution.py:110
  337.3 8.4 %gather_fusion.2 = f32[7,9,64,64]{3,2,1,0:T(8,128)} fusion(f32[9,64,64,8,8]{2,1,4,3,0:T(8,128)} %bitcast.364, s32[7]{0:T(128)S(1)} %copy-done.48), kind=kCustom, calls=%fused_computation.clone | custom fusion | bytes 2064440 | tf_op jit(solution)/shard_map/jit(diagonal)/gather | solution.py:110
  345.7 8.4 %gather_fusion.4 = f32[7,9,64,64]{3,2,1,0:T(8,128)} fusion(f32[9,64,64,8,8]{2,1,4,3,0:T(8,128)} %bitcast.367, s32[7]{0:T(128)S(1)} %copy-done.48), kind=kCustom, calls=%fused_computation.2.clone | custom fusion | bytes 2064440 | tf_op jit(solution)/shard_map/jit(diagonal)/gather | solution.py:110
  354.3 2.7 bitcast_reduce_fusion.3
  357.3 2.8 reduce_sum.78
  360.1 2.7 reduce_sum.81
  368.0 5.6 pad_add_fusion
  373.6 52.0 %all-reduce.16.cloned.1.call-done = (f32[27,64,64]{2,1,0:T(8,128)}, f32[27,64,64]{2,1,0:T(8,128)}) async-done(((f32[27,64,64]{2,1,0:T(8,128)}, f32[27,64,64]{2,1,0:T(8,128)}), (f32[27,64,64]{2,1,0:T(8,128)}, f32[27,64,64]{2,1,0:T(8,128)})) %all-reduce.16.cloned.1.call-update) | async-done | bytes 884752 | tf_op jit(solution)/shard_map/psum | solution.py:37
  427.1 27.6 %while.24 = (s32[]{:T(128)}, bf16[16,64,512]{2,1,0:T(8,128)(2,1)}, f32[20,68,512]{2,1,0:T(8,128)S(1)}, s32[4]{0:T(128)S(1)}, bf16[4,8,8,512]{3,2,1,0:T(8,128)(2,...) while((s32[]{:T(128)}, bf16[16,64,512]{2,1,0:T(8,128)(2,1)}, ...), condition=%wide.region_5.6_spmd, body=%wide.region_4.5_spmd.sunk | while | flops 204833 | bytes 1671694 | solution.py:246
  456.1 25.7 %all-reduce.14.cloned.1.call-done = (f32[27,64,64]{2,1,0:T(8,128)}, f32[27,64,64]{2,1,0:T(8,128)}) async-done(((f32[27,64,64]{2,1,0:T(8,128)}, f32[27,64,64]{2,1,0:T(8,128)}), (f32[27,64,64]{2,1,0:T(8,128)}, f32[27,64,64]{2,1,0:T(8,128)})) %all-reduce.14.cloned.1.call-update) | async-done | bytes 884752 | tf_op jit(solution)/shard_map/psum | solution.py:37
  482.9 2.6 collective-permute-start.8
  485.9 3.0 collective-permute-start.9
  492.8 44.6 %all-reduce.12.cloned.1.call-done = (f32[27,64,64]{2,1,0:T(8,128)}, f32[27,64,64]{2,1,0:T(8,128)}) async-done(((f32[27,64,64]{2,1,0:T(8,128)}, f32[27,64,64]{2,1,0:T(8,128)}), (f32[27,64,64]{2,1,0:T(8,128)}, f32[27,64,64]{2,1,0:T(8,128)})) %all-reduce.12.cloned.1.call-update) | async-done | bytes 884752 | tf_op jit(solution)/shard_map/psum | solution.py:37
  539.3 3.2 collective-permute-start.11
  546.1 20.5 %all-reduce.18.cloned.1.call-done = (f32[27,64,64]{2,1,0:T(8,128)}, f32[27,64,64]{2,1,0:T(8,128)}) async-done(((f32[27,64,64]{2,1,0:T(8,128)}, f32[27,64,64]{2,1,0:T(8,128)}), (f32[27,64,64]{2,1,0:T(8,128)}, f32[27,64,64]{2,1,0:T(8,128)})) %all-reduce.18.cloned.1.call-update) | async-done | bytes 884752 | tf_op jit(solution)/shard_map/psum | solution.py:37
  (354 shorter events, 197.5 us)
Async XLA Ops:
  7.2 418.4 %all-reduce.16.cloned.1.call-start = ((), (), s32[]{:S(2)}) async-start(), calls=%async_computation.2 | async-start | bytes 3538944 | tf_op jit(solution)/shard_map/psum | solution.py:37
  8.0 90.4 %collective-permute-start.5 = (bf16[2,64,8]{1,2,0:T(8,128)(2,1)S(1)}, bf16[2,64,8]{1,2,0:T(8,128)(2,1)S(1)}, u32[]{:S(2)}, u32[]{:S(2)}) collective-permute-start(bf16[2,64,8]{1,2,0:T(8,128)(2,1)S(1)} %get-tuple-element.364), channel_id=1, source_target_pairs={{8,0},{16,8},{24,16},{32,24},{40,32},{48,40},{56,48},{64,56},{72,6... | collective-permute-start | bytes 6152 | tf_op jit(solution)/shard_map/ppermute | solution.py:31
  9.3 89.1 %collective-permute-start.4 = (bf16[2,64,8]{1,2,0:T(8,128)(2,1)S(1)}, bf16[2,64,8]{1,2,0:T(8,128)(2,1)S(1)}, u32[]{:S(2)}, u32[]{:S(2)}) collective-permute-start(bf16[2,64,8]{1,2,0:T(8,128)(2,1)S(1)} %get-tuple-element.363), channel_id=1, source_target_pairs={{0,8},{8,16},{16,24},{24,32},{32,40},{40,48},{48,56},{56,64},{64,7... | collective-permute-start | bytes 6152 | tf_op jit(solution)/shard_map/ppermute | solution.py:30
  16.6 3.3 copy-start.43
  19.9 11.6 %copy-start.3 = (bf16[16,64,512]{2,1,0:T(8,128)(2,1)}, bf16[16,64,512]{2,1,0:T(8,128)(2,1)S(1)}, u32[]{:S(2)}) copy-start(bf16[16,64,512]{2,1,0:T(8,128)(2,1)S(1)} %reshape.660) | copy-start | bytes 3145732
  20.0 6.6 %copy-start.52 = (s32[16,64]{1,0:T(8,128)S(1)}, s32[16,64]{1,0:T(8,128)}, u32[]{:S(2)}) copy-start(s32[16,64]{1,0:T(8,128)} %param.25) | copy-start | bytes 12292
  20.0 6.6 %copy-start.53 = (s32[16,64]{1,0:T(8,128)S(1)}, s32[16,64]{1,0:T(8,128)}, u32[]{:S(2)}) copy-start(s32[16,64]{1,0:T(8,128)} %param.24) | copy-start | bytes 12292
  21.0 108.4 %collective-permute-start.1 = (bf16[2,64,512]{2,1,0:T(8,128)(2,1)}, bf16[2,64,512]{2,1,0:T(8,128)(2,1)S(1)}, u32[]{:S(2)}, u32[]{:S(2)}) collective-permute-start(bf16[2,64,512]{2,1,0:T(8,128)(2,1)} %get-tuple-element.352), channel_id=1, source_target_pairs={{8,0},{16,8},{24,16},{32,24},{40,32},{48,40},{56,48},{64,56},{72,6... | collective-permute-start | bytes 393224 | tf_op jit(solution)/shard_map/ppermute | solution.py:31
  22.3 107.1 %collective-permute-start = (bf16[2,64,512]{2,1,0:T(8,128)(2,1)}, bf16[2,64,512]{2,1,0:T(8,128)(2,1)S(1)}, u32[]{:S(2)}, u32[]{:S(2)}) collective-permute-start(bf16[2,64,512]{2,1,0:T(8,128)(2,1)} %get-tuple-element.351), channel_id=1, source_target_pairs={{0,8},{8,16},{16,24},{24,32},{32,40},{40,48},{48,56},{56,64},{64,7... | collective-permute-start | bytes 393224 | tf_op jit(solution)/shard_map/ppermute | solution.py:30
  29.1 3.6 copy-start.64
  56.9 8.2 %copy-start.60 = (f32[64]{0:T(128)S(1)}, f32[64]{0:T(128)}, u32[]{:S(2)}) copy-start(f32[64]{0:T(128)} %param.30) | copy-start | bytes 772
  79.9 6.6 %copy-start.61 = (f32[64]{0:T(128)S(1)}, f32[64]{0:T(128)}, u32[]{:S(2)}) copy-start(f32[64]{0:T(128)} %param.29) | copy-start | bytes 772
  79.9 7.2 %copy-start.62 = (f32[64]{0:T(128)S(1)}, f32[64]{0:T(128)}, u32[]{:S(2)}) copy-start(f32[64]{0:T(128)} %param.28) | copy-start | bytes 772
  82.5 7.2 %copy-start.63 = (f32[64]{0:T(128)S(1)}, f32[64]{0:T(128)}, u32[]{:S(2)}) copy-start(f32[64]{0:T(128)} %param.31) | copy-start | bytes 772
  89.7 72.5 %copy-start.21 = (bf16[512,512,1,1]{1,0,2,3:T(8,128)(2,1)}, bf16[512,512,1,1]{1,0,2,3:T(8,128)(2,1)S(1)}, u32[]{:S(2)}) copy-start(bf16[512,512,1,1]{1,0,2,3:T(8,128)(2,1)S(1)} %reshape.803) | copy-start | bytes 1572868
  98.4 20.6 %collective-permute-start.7 = (bf16[20,2,8]{1,2,0:T(8,128)(2,1)S(1)}, bf16[20,2,8]{1,2,0:T(8,128)(2,1)S(1)}, u32[]{:S(2)}, u32[]{:S(2)}) collective-permute-start(bf16[20,2,8]{1,2,0:T(8,128)(2,1)S(1)} %get-tuple-element.362), channel_id=1, source_target_pairs={{1,0},{2,1},{3,2},{4,3},{5,4},{6,5},{7,6},{9,8},{10,9},{11,10},{12... | collective-permute-start | bytes 1928 | tf_op jit(solution)/shard_map/ppermute | solution.py:31
  101.7 17.4 %collective-permute-start.6 = (bf16[20,2,8]{1,2,0:T(8,128)(2,1)S(1)}, bf16[20,2,8]{1,2,0:T(8,128)(2,1)S(1)}, u32[]{:S(2)}, u32[]{:S(2)}) collective-permute-start(bf16[20,2,8]{1,2,0:T(8,128)(2,1)S(1)} %get-tuple-element.361), channel_id=1, source_target_pairs={{0,1},{1,2},{2,3},{3,4},{4,5},{5,6},{6,7},{8,9},{9,10},{10,11},{11... | collective-permute-start | bytes 1928 | tf_op jit(solution)/shard_map/ppermute | solution.py:30
  112.5 6.7 %copy-start.51 = (bf16[4,10,10,8]{2,3,1,0:T(8,128)(2,1)S(1)}, bf16[4,10,10,8]{2,3,1,0:T(8,128)(2,1)}, u32[]{:S(2)}) copy-start(bf16[4,10,10,8]{2,3,1,0:T(8,128)(2,1)} %custom-call.19) | copy-start | bytes 19204
  117.7 18.1 %copy-start.56 = (bf16[4]{0:T(256)(128)(2,1)S(1)}, bf16[4]{0:T(256)(128)(2,1)}, u32[]{:S(2)}) copy-start(bf16[4]{0:T(256)(128)(2,1)} %compare_convert_fusion) | copy-start | bytes 28
  129.5 6.3 %copy-start.46 = (bf16[2,64,512]{2,1,0:T(8,128)(2,1)}, bf16[2,64,512]{2,1,0:T(8,128)(2,1)S(1)}, u32[]{:S(2)}) copy-start(bf16[2,64,512]{2,1,0:T(8,128)(2,1)S(1)} %collective-permute-done) | copy-start | bytes 393220
  130.2 7.9 %collective-permute-start.3 = (bf16[20,2,512]{2,1,0:T(2,128)(2,1)}, bf16[20,2,512]{2,1,0:T(2,128)(2,1)}, u32[]{:S(2)}, u32[]{:S(2)}) collective-permute-start(bf16[20,2,512]{2,1,0:T(2,128)(2,1)} %get-tuple-element.350), channel_id=1, source_target_pairs={{1,0},{2,1},{3,2},{4,3},{5,4},{6,5},{7,6},{9,8},{10,9},{11,10},{12... | collective-permute-start | bytes 122888 | tf_op jit(solution)/shard_map/ppermute | solution.py:31
  132.1 6.0 %collective-permute-start.2 = (bf16[20,2,512]{2,1,0:T(2,128)(2,1)}, bf16[20,2,512]{2,1,0:T(2,128)(2,1)}, u32[]{:S(2)}, u32[]{:S(2)}) collective-permute-start(bf16[20,2,512]{2,1,0:T(2,128)(2,1)} %get-tuple-element.349), channel_id=1, source_target_pairs={{0,1},{1,2},{2,3},{3,4},{4,5},{5,6},{6,7},{8,9},{9,10},{10,11},{11... | collective-permute-start | bytes 122888 | tf_op jit(solution)/shard_map/ppermute | solution.py:30
  136.7 1.4 copy-start.47
  138.1 15.4 %copy-start.57 = (bf16[4]{0:T(256)(128)(2,1)S(1)}, bf16[4]{0:T(256)(128)(2,1)}, u32[]{:S(2)}) copy-start(bf16[4]{0:T(256)(128)(2,1)} %compare_convert_fusion) | copy-start | bytes 28
  139.8 15.1 %copy-start.23 = (bf16[512,512,1,1]{1,0,2,3:T(8,128)(2,1)S(1)}, bf16[512,512,1,1]{1,0,2,3:T(8,128)(2,1)}, u32[]{:S(2)}) copy-start(bf16[512,512,1,1]{1,0,2,3:T(8,128)(2,1)} %reshape.795) | copy-start | bytes 1572868
  153.5 1.9 copy-start.32
  162.3 1.1 copy-start.39
  163.5 1.3 copy-start.25
  164.0 1.1 copy-start.24
  167.4 1.1 copy-start.66
  240.5 3.5 copy-start.17
  244.0 2.2 copy-start.15
  246.2 2.2 copy-start.13
  248.3 2.2 copy-start.11
  250.5 2.2 copy-start.9
  252.7 2.2 copy-start.7
  254.9 2.2 copy-start.5
  257.1 1.7 copy-start.49
  258.8 7.1 %copy-start.50 = (s32[8]{0:T(128)S(1)}, s32[8]{0:T(128)}, u32[]{:S(2)}) copy-start(s32[8]{0:T(128)} %or_bitcast_fusion.2) | copy-start | bytes 100
  302.2 3.5 copy-start.18
  305.7 2.2 copy-start.16
  307.9 2.2 copy-start.14
  310.1 2.2 copy-start.12
  312.2 2.2 copy-start.10
  314.4 2.2 copy-start.8
  316.6 2.2 copy-start.6
  328.8 8.5 %copy-start.48 = (s32[7]{0:T(128)S(1)}, s32[7]{0:T(128)}, u32[]{:S(2)}) copy-start(s32[7]{0:T(128)} %get-tuple-element.379) | copy-start | bytes 88
  354.1 2.9 copy-start
  357.3 5.5 copy-start.1
  362.7 2.0 copy-start.41
  365.8 1.9 copy-start.19
  365.8 1.9 copy-start.22
  365.8 116.0 %all-reduce.14.cloned.1.call-start = ((), (), s32[]{:S(2)}) async-start(), calls=%async_computation.1 | async-start | bytes 3538944 | tf_op jit(solution)/shard_map/psum | solution.py:37
  365.8 2.1 copy-start.20
  425.6 1.5 copy-start.65
  425.6 111.8 %all-reduce.12.cloned.1.call-start = ((), (), s32[]{:S(2)}) async-start(), calls=%async_computation | async-start | bytes 3538944 | tf_op jit(solution)/shard_map/psum | solution.py:37
  481.8 84.7 %all-reduce.18.cloned.1.call-start = ((), (), s32[]{:S(2)}) async-start(), calls=%async_computation.3 | async-start | bytes 3538944 | tf_op jit(solution)/shard_map/psum | solution.py:37
  482.9 6.0 %collective-permute-start.8 = (bf16[20,2,512]{2,1,0:T(2,128)(2,1)S(1)}, bf16[20,2,512]{2,1,0:T(2,128)(2,1)S(1)}, u32[]{:S(2)}, u32[]{:S(2)}) collective-permute-start(bf16[20,2,512]{2,1,0:T(2,128)(2,1)S(1)} %get-tuple-element.346), channel_id=1, source_target_pairs={{1,0},{2,1},{3,2},{4,3},{5,4},{6,5},{7,6},{9,8},{10,9},{11,10},{12... | collective-permute-start | bytes 122888 | tf_op jit(solution)/shard_map/ppermute | solution.py:20
  485.9 4.1 collective-permute-start.9
  490.1 1.5 copy-start.2
  491.6 51.0 %collective-permute-start.10 = (bf16[2,64,512]{2,1,0:T(8,128)(2,1)S(1)}, bf16[2,64,512]{2,1,0:T(8,128)(2,1)S(1)}, u32[]{:S(2)}, u32[]{:S(2)}) collective-permute-start(bf16[2,64,512]{2,1,0:T(8,128)(2,1)S(1)} %get-tuple-element.348), channel_id=1, source_target_pairs={{8,0},{16,8},{24,16},{32,24},{40,32},{48,40},{56,48},{64,56},{72,6... | collective-permute-start | bytes 393224 | tf_op jit(solution)/shard_map/ppermute | solution.py:20
  537.4 7.3 %copy-start.4 = (bf16[16,64,512]{2,1,0:T(8,128)(2,1)S(1)}, bf16[16,64,512]{2,1,0:T(8,128)(2,1)}, u32[]{:S(2)}) copy-start(bf16[16,64,512]{2,1,0:T(8,128)(2,1)} %copy-done.3) | copy-start | bytes 3145732
  539.3 5.4 collective-permute-start.11
  566.5 2.3 copy-start.44
  (19 other events, 19.3 us)
Sparse Core Ops, SparseCore 0:
  365.9 59.5 all-reduce.15
  428.1 53.6 all-reduce.13
  484.2 53.1 all-reduce.11
  539.9 26.5 all-reduce.17
where the time goes:
time: 583 us; the launch traced here: 577 us
  local copies, waits for them, and re-layouts  262 us (45%)
  waiting for transfers between devices  145 us (25%)
  matrix products  59.2 us (10%)
  other arithmetic  50.1 us (9%)
  starting transfers between devices  34 us (6%)
  between operations  15.1 us (3%)
  loops' own time  11.3 us (2%)
    psum x4, waiting for transfers between devices, over_axes(): return functools.reduce(lax.psum, axes, array)  143 us
    another operation x20, local copies, waits for them, and re-layouts, weight_grad(): return jnp.stack(products)  51.8 us
    unnamed x153, local copies, waits for them, and re-layouts  49.4 us
    gather x6, local copies, waits for them, and re-layouts, fold_banded(): jnp.diagonal(blocks, offset=1 - lift_index, axis1=1, axis2=3)  49.1 us
    squeeze x18, local copies, waits for them, and re-layouts, forward_conv(): running = running + flat_dot(window, banded[offset])  43.2 us
    gather x36, local copies, waits for them, and re-layouts  37.3 us
    dot_general x18, matrix products, adjoint_conv(): lax.dot_general(window.reshape(-1, width), banded[offset], (((1,), (1,)),...  25.3 us
    dot_general x18, matrix products, weight_grad(): lax.dot_general(window, flat_errors, (((0,), (0,)), ((), ())), preferred_...  25.2 us
  transfers between devices with their start and end apart: 16, of which 6 were waited for; matrix products, arithmetic and copies ran while one was open for 24% of the time, Pallas kernels for 0%

commit v1 on v0

v1 whole, which is shorter than its diff:
```python
import functools

import jax
import jax.numpy as jnp
from jax import lax
from jax.experimental import pallas as pl
from jax.experimental.pallas import tpu as pltpu
from jax.sharding import PartitionSpec as P

MESH = pl.DeviceIdType.MESH
F32 = jnp.float32
BF16 = jnp.bfloat16
BRICK = 8
C = 64
WIDTH = 512
SLOTS = 4
SHARE = 2
BX, BY = 2, 8
W = 12
ROWS = SLOTS * W
CORE = SLOTS * BRICK
BLOCKS = 16
HALOS = [(dx, dy) for dx in (-1, 0, 1) for dy in (-1, 0, 1) if dx or dy]


def lane(shape):
    return lax.broadcasted_iota(jnp.int32, shape, len(shape) - 1)


def turned(value):
    return pltpu.roll(value, 64, value.ndim - 1)


def height_mask(bounds):
    first = lane(bounds.shape) < 64
    other = turned(bounds)
    low, high = jnp.where(first, bounds, other), jnp.where(first, other, bounds)
    step = jnp.where(first, 0.0, 1.0)
    return [(step + 2.0 * c >= low) & (step + 2.0 * c < high) for c in range(4)]


def toeplitz(one, two, pair_ref, t):
    first = lane(one.shape) < 64
    zero = jnp.zeros_like(one)
    start = jnp.where(first, turned(one), zero)
    end = jnp.where(first, zero, turned(two))
    whole = [zero, start, one, two, end, zero]
    columns = (
        ([one, two, end, zero, zero, zero], whole),
        (whole, [zero, zero, zero, start, one, two]),
    )
    rows = pl.ds(pl.multiple_of(t * 384, 384), 384)
    for g in range(2):
        for c in range(2):
            block = jnp.concatenate(columns[g][c], axis=0).astype(BF16)
            pair_ref[g, rows, 128 * c : 128 * c + 128] = block


def build_weights(w_ref, forward_ref, adjoint_ref):
    def tap(t, carry):
        rows = w_ref[pl.ds(pl.multiple_of(t * 192, 192), 192), :].astype(F32)
        lower, middle, upper = rows[:64], rows[64:128], rows[128:]
        toeplitz(
            jnp.concatenate([middle, lower], axis=1),
            jnp.concatenate([upper, middle], axis=1),
            forward_ref,
            t,
        )
        toeplitz(rows[64:192].T, rows[0:128].T, adjoint_ref, 8 - t)
        return carry

    lax.fori_loop(0, 9, tap, 0)


def conv(source, pair_ref, g, start, count, pitch):
    lanes = slice(128 * g, 128 * g + 384)
    parts = [
        source[oy, start + ox * pitch : start + ox * pitch + count, lanes]
        for ox in range(3)
        for oy in range(3)
    ]
    return jnp.dot(
        jnp.concatenate(parts, axis=1), pair_ref[g], preferred_element_type=F32
    )


def shifted(value):
    count = value.shape[0]
    return (pltpu.roll(value, 1, 0), value, pltpu.roll(value, count - 1, 0))


def fold(results, fold_ref, t0):
    for oy in range(3):
        sums = {}
        for g in range(2):
            for z in range(4 * g, 4 * g + 4):
                for c in range(3):
                    kind = (z % 2, 2 * g + 2 * c - z)
                    if kind in ((0, 0), (0, -2), (1, -1), (1, 1)):
                        zo = z - 4 * g
                        block = results[g][
                            64 * zo : 64 * zo + 64,
                            384 * oy + 128 * c : 384 * oy + 128 * c + 128,
                        ]
                        sums[kind] = sums[kind] + block if kind in sums else block
        p, u, q, s = sums[0, 0], sums[0, -2], sums[1, -1], sums[1, 1]
        first = lane(p.shape) < 64
        fold_ref[t0 + oy] = q + turned(jnp.where(first, p, u))
        fold_ref[9 + t0 + oy] = p + turned(s)


def weight_sums(errors_t, source, start, count, pitch, fold_ref, block_ref):
    def column(ox, carry):
        base = pl.multiple_of(start + ox * pitch, 16)
        results = []
        for g in range(2):
            lanes = slice(128 * g, 128 * g + 384)
            window = jnp.concatenate(
                [source[oy, pl.ds(base, count), lanes] for oy in range(3)], axis=1
            )
            results.append(
                jnp.dot(errors_t[g], window, preferred_element_type=F32)
            )
        fold(results, fold_ref, 3 * ox)
        return carry

    lax.fori_loop(0, 3, column, 0)
    first = lane((64, 128)) < 64
    for t in range(9):
        block_ref[t] = fold_ref[t].astype(BF16)
    for i in range(5):
        even = turned(fold_ref[9 + 2 * i])
        odd = fold_ref[10 + 2 * i] if i < 4 else jnp.zeros_like(even)
        block_ref[9 + i] = jnp.where(first, even, odd).astype(BF16)
    block_ref[14] = jnp.zeros((64, 128), BF16)
    block_ref[15] = jnp.zeros((64, 128), BF16)


def unfold(blocks_ref, per, out_ref, factor):
    for t in range(9):
        block = blocks_ref[t // per, t % per].astype(F32) * factor
        out_ref[192 * t : 192 * t + 128, :] = block.T
    for i in range(5):
        block = (blocks_ref[(9 + i) // per, (9 + i) % per].astype(F32) * factor).T
        out_ref[384 * i + 128 : 384 * i + 192, :] = block[:64]
        if i < 4:
            out_ref[384 * i + 320 : 384 * i + 384, :] = block[64:]


def block_kernel(
    n_gx,
    n_gy,
    feat,
    bounds,
    cot,
    low,
    high,
    w_one,
    w_two,
    par,
    out,
    gfeat,
    gw_one,
    gw_two,
    ext,
    elh,
    pick_in,
    pick_bounds,
    pick_target,
    put_out,
    put_grad,
    src_one,
    src_two,
    err_two,
    err_one,
    msk,
    core_in,
    core_mask,
    target,
    slope,
    frame,
    res,
    grad_region,
    gsum,
    fwd_one,
    adj_one,
    fwd_two,
    adj_two,
    folded,
    blocks,
    got_x,
    half,
    got_y,
    full,
    out_x,
    in_x,
    out_y,
    in_y,
    out_c,
    in_c,
    local_sem,
    halo_send,
    halo_recv,
    edge_send,
    edge_recv,
    sum_send,
    sum_recv,
):
    comm = n_gx * n_gy > 1
    if comm:
        gx, gy = lax.axis_index("gx"), lax.axis_index("gy")
    else:
        gx, gy = 0, 0
    nx, ny = feat.shape[0], feat.shape[1]
    per = BLOCKS // n_gx

    def device(dx, dy):
        return (lax.rem(gx + dx + n_gx, n_gx), lax.rem(gy + dy + n_gy, n_gy))

    if comm:
        barrier = pltpu.get_barrier_semaphore()
        peers = [(d, 0) for d in range(1, n_gx)] + [(0, d) for d in range(1, n_gy)]
        peers += [(dx, dy) for dx, dy in HALOS if dx and dy]
        for dx, dy in peers:
            pl.semaphore_signal(
                barrier, inc=1, device_id=device(dx, dy), device_id_type=MESH
            )
        pl.semaphore_wait(barrier, len(peers))

    def remote(src, dst, send, recv, to):
        return pltpu.make_async_remote_copy(
            src_ref=src,
            dst_ref=dst,
            send_sem=send,
            recv_sem=recv,
            device_id=to,
            device_id_type=MESH,
        )

    halos = []
    if comm:
        x_from = {-1: slice(0, 2), 0: slice(0, nx), 1: slice(nx - 2, nx)}
        x_to = {-1: slice(nx + 2, nx + 4), 0: slice(2, nx + 2), 1: slice(0, 2)}
        y_from = {-1: slice(0, 16), 0: slice(0, ny), 1: slice(ny - 16, ny)}
        y_to = {-1: slice(ny + 16, ny + 32), 0: slice(16, ny + 16), 1: slice(0, 16)}
        order = sorted(HALOS, key=lambda h: -(2 * abs(h[0]) - abs(h[1])))
        for i, (dx, dy) in enumerate(order):
            for k, (src, dst) in enumerate(((feat, ext), (bounds, elh))):
                copy = remote(
                    src.at[x_from[dx], y_from[dy]],
                    dst.at[x_to[dx], y_to[dy]],
                    halo_send.at[k, i],
                    halo_recv.at[k, i],
                    device(dx, dy),
                )
                copy.start()
                halos.append(copy)
    own = [
        pltpu.make_async_copy(
            src, dst.at[2 : nx + 2, 16 : ny + 16], local_sem.at[k]
        )
        for k, (src, dst) in enumerate(((feat, ext), (bounds, elh)))
    ]
    for copy in own:
        copy.start()

    build_weights(w_one, fwd_one, adj_one)
    build_weights(w_two, fwd_two, adj_two)
    nothing = jnp.zeros((3, 2 * ROWS, WIDTH), BF16)
    err_two[:, 0 : 2 * ROWS, :] = nothing
    err_two[:, 10 * ROWS : 12 * ROWS, :] = nothing
    err_one[:, 0 : 2 * ROWS, :] = nothing
    err_one[:, 12 * ROWS : 14 * ROWS, :] = nothing
    frame[...] = jnp.zeros_like(frame)

    occupied = jnp.where(high[...] > low[...], 1, 0)
    by_lane = lane((8, ny))
    count = jnp.int32(0)
    brick = [jnp.int32(-1000)] * SLOTS
    for bx in range(BX):
        rows = occupied[8 * bx : 8 * bx + 8]
        for by in range(BY):
            inside = (by_lane >= 8 * by) & (by_lane < 8 * by + 8)
            filled = jnp.max(jnp.where(inside, rows, 0))
            for j in range(SLOTS):
                hit = (filled > 0) & (count == j)
                brick[j] = jnp.where(hit, 8 * bx + by, brick[j])
            count = count + filled

    def picks(rows, columns, row_dim, per_brick, pitch, offset):
        shape = (rows, columns) if row_dim == 0 else (columns, rows)
        row = lax.broadcasted_iota(jnp.int32, shape, row_dim)
        column = lax.broadcasted_iota(jnp.int32, shape, 1 - row_dim)
        wanted = row + offset
        for j in range(SLOTS):
            b = brick[j]
            bx = jnp.where(b >= BY, 1, 0)
            spot = jnp.where(b < 0, -4000, bx * pitch + 8 * (b - BY * bx)) - per_brick * j
            inside = (row >= per_brick * j) & (row < per_brick * j + per_brick)
            wanted = wanted + jnp.where(inside, spot, 0)
        return jnp.where(column == wanted, 1.0, 0.0).astype(BF16)

    tall = ny + 32
    core_pick = picks(CORE, 2 * tall, 0, BRICK, tall, 16)
    frame_pick = [picks(ROWS, 2 * tall, 0, W, tall, 13 + oy) for oy in range(3)]
    pick_in[...] = jnp.concatenate(frame_pick + [core_pick], axis=0)
    pick_bounds[...] = jnp.concatenate([frame_pick[1], core_pick], axis=0)
    pick_target[...] = picks(CORE, 2 * ny, 0, BRICK, ny, 0)
    put_out[...] = picks(CORE, 2 * ny, 1, BRICK, ny, 0)
    put_grad[...] = picks(ROWS, 2 * (ny + 16), 1, W, ny + 16, 6)

    def cut_target(x, carry):
        rows = jnp.concatenate([cot[x], cot[8 + x]], axis=0)
        spot = pl.ds(pl.multiple_of(x * CORE, CORE), CORE)
        target[spot, :] = jnp.dot(pick_target[...], rows, preferred_element_type=F32)
        return carry

    lax.fori_loop(0, 8, cut_target, 0)

    def mask_in(x, y0, n):
        mask = height_mask(elh[x, y0 : y0 + n, :].astype(F32))
        for c in range(4):
            lanes = slice(128 * c, 128 * c + 128)
            value = ext[x, y0 : y0 + n, lanes].astype(F32)
            ext[x, y0 : y0 + n, lanes] = jnp.where(mask[c], value, 0.0).astype(BF16)

    def mask_rows(*spots):
        def one(x, carry):
            for y0, n in spots:
                mask_in(x, y0, n)
            return carry

        return one

    for copy in own:
        copy.wait()
    lax.fori_loop(2, nx + 2, mask_rows((16, ny)), 0)
    for copy in halos:
        copy.wait()
    if comm:
        for spot, inside in (
            ((slice(0, 2), slice(None)), gx > 0),
            ((slice(nx + 2, nx + 4), slice(None)), gx < n_gx - 1),
            ((slice(None), slice(0, 16)), gy > 0),
            ((slice(None), slice(ny + 16, ny + 32)), gy < n_gy - 1),
        ):
            value = elh[spot[0], spot[1], :].astype(F32)
            elh[spot[0], spot[1], :] = (
                value * jnp.where(inside, 1.0, 0.0).astype(F32)
            ).astype(BF16)
    else:
        for spot in (slice(0, 2), slice(nx + 2, nx + 4)):
            elh[spot] = jnp.zeros_like(elh[spot])
            ext[spot] = jnp.zeros_like(ext[spot])
        for spot in (slice(0, 16), slice(ny + 16, ny + 32)):
            elh[:, spot] = jnp.zeros_like(elh[:, spot])
            ext[:, spot] = jnp.zeros_like(ext[:, spot])

    lax.fori_loop(2, nx + 2, mask_rows((0, 16), (ny + 16, 16)), 0)
    for x in (0, nx + 2):
        lax.fori_loop(x, x + 2, mask_rows((0, tall)), 0)

    def cut(x, carry):
        base = pl.multiple_of(x * ROWS, ROWS)
        core = pl.multiple_of(x * CORE, CORE)
        rows = jnp.concatenate([ext[x], ext[8 + x]], axis=0)
        value = jnp.dot(pick_in[...], rows, preferred_element_type=F32)
        for oy in range(3):
            src_one[oy, pl.ds(base, ROWS), :] = value[
                ROWS * oy : ROWS * oy + ROWS
            ].astype(BF16)
        core_in[pl.ds(core, CORE), :] = value[3 * ROWS :]
        rows = jnp.concatenate([elh[x], elh[8 + x]], axis=0)
        mask = height_mask(
            jnp.dot(pick_bounds[...], rows, preferred_element_type=F32)
        )
        for c in range(4):
            lanes = slice(128 * c, 128 * c + 128)
            value = jnp.where(mask[c], 1.0, 0.0)
            msk[pl.ds(base, ROWS), lanes] = value[:ROWS]
            core_mask[pl.ds(core, CORE), lanes] = value[ROWS:]
        return carry

    lax.fori_loop(0, W, cut, 0)

    scale_one, shift_one = par[0:1, :], par[1:2, :]
    scale_two, shift_two = par[2:3, :], par[3:4, :]

    for g in range(2):
        lanes = slice(256 * g, 256 * g + 256)
        pre = conv(src_one, fwd_one, g, 0, 10 * ROWS, ROWS) * scale_one + shift_one
        s = jax.nn.sigmoid(pre)
        mask = msk[ROWS : 11 * ROWS, lanes]
        hidden = pre * s * mask
        slope[:, lanes] = s * (1.0 + pre * (1.0 - s)) * mask * scale_one
        for x in range(10):
            rows = hidden[ROWS * x : ROWS * x + ROWS]
            for oy in range(3):
                for j in range(0, SLOTS, 2):
                    both = [
                        rows[W * i + 1 + oy : W * i + 9 + oy] for i in (j, j + 1)
                    ]
                    src_two[oy, CORE * x + 8 * j : CORE * x + 8 * j + 16, lanes] = (
                        jnp.concatenate(both, axis=0).astype(BF16)
                    )

    middle = slice(2 * CORE, 10 * CORE)
    errors_t = []
    for g in range(2):
        lanes = slice(256 * g, 256 * g + 256)
        pre = conv(src_two, fwd_two, g, 0, 8 * CORE, CORE) * scale_two + shift_two
        pre = pre + core_in[middle, lanes]
        s = jax.nn.sigmoid(pre)
        mask = core_mask[middle, lanes]
        result = pre * s * mask
        grad = target[:, lanes] * mask * (s * (1.0 + pre * (1.0 - s)))
        errors_t.append((grad * scale_two).T.astype(BF16))
        res[:, lanes] = result.astype(BF16)
        for x in range(8):
            for j in range(SLOTS):
                spot = CORE * x + 8 * j
                frame[x, W * j + 2 : W * j + 10, lanes] = grad[spot : spot + 8]

    def spread(x, carry):
        base = pl.multiple_of((x + 2) * ROWS, ROWS)
        for g in range(2):
            lanes = slice(256 * g, 256 * g + 256)
            for oy, moved in enumerate(shifted(frame[x, :, lanes] * scale_two)):
                err_two[oy, pl.ds(base, ROWS), lanes] = moved.astype(BF16)
        return carry

    lax.fori_loop(0, 8, spread, 0)

    def exchange(conv_id):
        copies = []
        for d in range(1, n_gx):
            to = lax.rem(gx + d, n_gx)
            copy = remote(
                blocks.at[conv_id, pl.ds(to * per, per)],
                got_x.at[conv_id, gx],
                sum_send.at[conv_id, 0, d],
                sum_recv.at[conv_id, 0, d],
                (to, gy),
            )
            copy.start()
            copies.append(copy)
        got_x[conv_id, gx] = blocks[conv_id, pl.ds(gx * per, per)]
        return copies

    def add_up(conv_id, copies, source, where, n):
        for copy in copies:
            copy.wait_recv()
        total = source[conv_id, 0].astype(F32)
        for s in range(1, n):
            total = total + source[conv_id, s].astype(F32)
        where[conv_id] = total.astype(BF16)
        return copies

    def exchange_y(conv_id):
        copies = []
        for d in range(1, n_gy):
            copy = remote(
                half.at[0, conv_id],
                got_y.at[conv_id, gy],
                sum_send.at[conv_id, 1, d],
                sum_recv.at[conv_id, 1, d],
                (gx, lax.rem(gy + d, n_gy)),
            )
            copy.start()
            copies.append(copy)
        got_y[conv_id, gy] = half[0, conv_id]
        return copies

    def gather(conv_id):
        copies = []
        for d in range(1, n_gx):
            copy = remote(
                half.at[1, conv_id],
                full.at[conv_id, gx],
                sum_send.at[conv_id, 2, d],
                sum_recv.at[conv_id, 2, d],
                (lax.rem(gx + d, n_gx), gy),
            )
            copy.start()
            copies.append(copy)
        full[conv_id, gx] = half[1, conv_id]
        return copies

    weight_sums(
        errors_t, src_two, 0, 8 * CORE, CORE, folded, blocks.at[1]
    )
    sent_two = exchange(1)

    errors_t = []
    for g in range(2):
        lanes = slice(256 * g, 256 * g + 256)
        back = conv(err_two, adj_two, g, 0, 10 * ROWS, ROWS)
        error = back * slope[:, lanes]
        errors_t.append(error.T.astype(BF16))
        for x in range(10):
            rows = error[ROWS * x : ROWS * x + ROWS]
            spot = slice(ROWS * (x + 2), ROWS * (x + 3))
            for oy, moved in enumerate(shifted(rows)):
                err_one[oy, spot, lanes] = moved.astype(BF16)
    weight_sums(errors_t, src_one, 0, 10 * ROWS, ROWS, folded, blocks.at[0])
    sent_one = exchange(0)
    add_up(1, sent_two, got_x, half.at[0], n_gx)
    sent_two_y = exchange_y(1)

    for g in range(2):
        lanes = slice(256 * g, 256 * g + 256)
        back = conv(err_one, adj_one, g, 0, 12 * ROWS, ROWS)
        for x in range(W):
            rows = back[ROWS * x : ROWS * x + ROWS]
            if 2 <= x < 10:
                rows = rows + frame[x - 2, :, lanes]
            grad_region[x, :, lanes] = rows.astype(BF16)

    add_up(0, sent_one, got_x, half.at[0], n_gx)
    sent_one_y = exchange_y(0)
    add_up(1, sent_two_y, got_y, half.at[1], n_gy)
    sent_two_full = gather(1)

    for bxs, start, stop in (((0,), 0, 8), ((0, 1), 8, W), ((1,), W, 20)):

        def collect(x, carry, bxs=bxs):
            total = None
            for bx in bxs:
                part = jnp.dot(
                    put_grad[bx * (ny + 16) : (bx + 1) * (ny + 16), :],
                    grad_region[x - 8 * bx],
                    preferred_element_type=F32,
                )
                total = part if total is None else total + part
            gsum[x] = total
            return carry

        lax.fori_loop(start, stop, collect, 0)

    edges = []
    if comm:
        out_x[0] = gsum[0:2, 8 : ny + 8, :].astype(BF16)
        out_x[1] = gsum[nx + 2 : nx + 4, 8 : ny + 8, :].astype(BF16)
        for side, t in enumerate((0, ny + 8)):
            for i in range(nx // 2):
                both = [gsum[2 + 2 * i + k, t : t + 8, :] for k in range(2)]
                out_y[side, i] = jnp.concatenate(both, axis=0).astype(BF16)
            for up, x in enumerate((0, nx + 2)):
                both = [gsum[x + k, t : t + 8, :] for k in range(2)]
                out_c[up, side] = jnp.concatenate(both, axis=0).astype(BF16)
        for i, (dx, dy) in enumerate(HALOS):
            a, b = (dx + 1) // 2, (dy + 1) // 2
            if dy == 0:
                src, dst = out_x.at[a], in_x.at[1 - a]
            elif dx == 0:
                src, dst = out_y.at[b], in_y.at[1 - b]
            else:
                src, dst = out_c.at[a, b], in_c.at[1 - a, 1 - b]
            copy = remote(
                src, dst, edge_send.at[i], edge_recv.at[i], device(dx, dy)
            )
            copy.start()
            edges.append(copy)

    def deposit(x, carry):
        rows = res[pl.ds(pl.multiple_of(x * CORE, CORE), CORE), :]
        value = jnp.dot(put_out[...], rows, preferred_element_type=F32).astype(BF16)
        out[x] = value[:ny]
        out[8 + x] = value[ny:]
        return carry

    lax.fori_loop(0, 8, deposit, 0)

    add_up(0, sent_one_y, got_y, half.at[1], n_gy)
    sent_one_full = gather(0)

    if comm:
        for copy in edges:
            copy.wait_recv()
        x_in = [
            jnp.where(inside, 1.0, 0.0).astype(F32)
            for inside in (gx > 0, gx < n_gx - 1)
        ]
        y_in = [
            jnp.where(inside, 1.0, 0.0).astype(F32)
            for inside in (gy > 0, gy < n_gy - 1)
        ]
        for a, x in enumerate((2, nx)):
            gsum[x : x + 2, 8 : ny + 8, :] += in_x[a].astype(F32) * x_in[a]
            for b, t in enumerate((8, ny)):
                rows = in_c[a, b].astype(F32) * (x_in[a] * y_in[b])
                for k in range(2):
                    gsum[x + k, t : t + 8, :] += rows[8 * k : 8 * k + 8]
        for b, t in enumerate((8, ny)):
            for i in range(nx // 2):
                rows = in_y[b, i].astype(F32) * y_in[b]
                for k in range(2):
                    gsum[2 + 2 * i + k, t : t + 8, :] += rows[8 * k : 8 * k + 8]

    def finish(x, carry):
        mask = height_mask(elh[x + 2, 16 : ny + 16, :].astype(F32))
        for c in range(4):
            lanes = slice(128 * c, 128 * c + 128)
            value = gsum[x + 2, 8 : ny + 8, lanes]
            gfeat[x, :, lanes] = jnp.where(mask[c], value, 0.0).astype(BF16)
        return carry

    lax.fori_loop(0, nx, finish, 0)

    for conv_id, copies, gw in ((1, sent_two_full, gw_two), (0, sent_one_full, gw_one)):
        for copy in copies:
            copy.wait_recv()
        unfold(full.at[conv_id], per, gw, 1.0 / (n_gx * n_gy * SHARE))
    for copies in (
        edges,
        sent_one,
        sent_two,
        sent_one_y,
        sent_two_y,
        sent_one_full,
        sent_two_full,
    ):
        for copy in copies:
            copy.wait_send()


def run(
    n_gx,
    n_gy,
    features,
    cotangent,
    low,
    high,
    weight_one,
    weight_two,
    scale_one,
    shift_one,
    scale_two,
    shift_two,
):
    nx, ny = features.shape[0], features.shape[1]
    per = BLOCKS // n_gx
    first = lax.broadcasted_iota(jnp.int32, (nx, ny, 128), 2) < 64
    bounds = jnp.where(first, low[..., None], high[..., None]).astype(BF16)
    par = jnp.stack(
        [jnp.tile(v, 4) for v in (scale_one, shift_one, scale_two, shift_two)]
    )
    whole = pl.BlockSpec(memory_space=pltpu.VMEM)
    left = pl.BlockSpec(memory_space=pl.ANY)
    vm = pltpu.VMEM
    dma = pltpu.SemaphoreType.DMA
    scratch = [
        vm((nx + 4, ny + 32, WIDTH), BF16),
        vm((nx + 4, ny + 32, 128), BF16),
        vm((3 * ROWS + CORE, 2 * ny + 64), BF16),
        vm((ROWS + CORE, 2 * ny + 64), BF16),
        vm((CORE, 2 * ny), BF16),
        vm((2 * ny, CORE), BF16),
        vm((2 * ny + 32, ROWS), BF16),
        vm((3, W * ROWS, WIDTH), BF16),
        vm((3, 10 * CORE, WIDTH), BF16),
        vm((3, W * ROWS, WIDTH), BF16),
        vm((3, (W + 2) * ROWS, WIDTH), BF16),
        vm((W * ROWS, WIDTH), F32),
        vm((W * CORE, WIDTH), F32),
        vm((W * CORE, WIDTH), F32),
        vm((8 * CORE, WIDTH), F32),
        vm((10 * ROWS, WIDTH), F32),
        vm((8, ROWS, WIDTH), F32),
        vm((8 * CORE, WIDTH), BF16),
        vm((W, ROWS, WIDTH), BF16),
        vm((nx + 4, ny + 16, WIDTH), F32),
        vm((2, 27 * 128, 256), BF16),
        vm((2, 27 * 128, 256), BF16),
        vm((2, 27 * 128, 256), BF16),
        vm((2, 27 * 128, 256), BF16),
        vm((18, 64, 128), F32),
        vm((2, BLOCKS, 64, 128), BF16),
        vm((2, n_gx, per, 64, 128), BF16),
        vm((2, 2, per, 64, 128), BF16),
        vm((2, n_gy, per, 64, 128), BF16),
        vm((2, n_gx, per, 64, 128), BF16),
        vm((2, 2, ny, WIDTH), BF16),
        vm((2, 2, ny, WIDTH), BF16),
        vm((2, nx // 2, 16, WIDTH), BF16),
        vm((2, nx // 2, 16, WIDTH), BF16),
        vm((2, 2, 16, WIDTH), BF16),
        vm((2, 2, 16, WIDTH), BF16),
        dma((2,)),
        dma((2, 8)),
        dma((2, 8)),
        dma((8,)),
        dma((8,)),
        dma((2, 3, 16)),
        dma((2, 3, 16)),
    ]
    comm = n_gx * n_gy > 1
    params = pltpu.CompilerParams(
        collective_id=0 if comm else None,
        has_side_effects=comm,
        vmem_limit_bytes=60 * 2**20,
    )
    out, gfeat, gw_one, gw_two = pl.pallas_call(
        functools.partial(block_kernel, n_gx, n_gy),
        out_shape=(
            jax.ShapeDtypeStruct(features.shape, BF16),
            jax.ShapeDtypeStruct(features.shape, BF16),
            jax.ShapeDtypeStruct((27 * C, C), F32),
            jax.ShapeDtypeStruct((27 * C, C), F32),
        ),
        in_specs=[left, left] + [whole] * 6,
        out_specs=(whole,) * 4,
        scratch_shapes=scratch,
        compiler_params=params,
        name="residual_block",
    )(
        features,
        bounds,
        cotangent,
        low,
        high,
        weight_one.reshape(27 * C, C),
        weight_two.reshape(27 * C, C),
        par,
    )
    return out, gfeat, gw_one.reshape(27, C, C), gw_two.reshape(27, C, C)


def solution(mesh):
    columns = P("gx", "gy", None)
    placed = (columns, columns, P("gx", "gy"), P("gx", "gy")) + (P(),) * 6
    return jax.shard_map(
        functools.partial(run, mesh.shape["gx"], mesh.shape["gy"]),
        mesh=mesh,
        in_specs=placed,
        out_specs=(columns, columns, P(), P()),
        check_vma=False,
    )
```

time: 583 us -> 71.2 us (0.12); the launches traced: 577 us -> 70.9 us
  local copies, waits for them, and re-layouts: 262 us -> 9.01 us
  waiting for transfers between devices: 145 us -> 0 us
  Pallas kernels: 0 us -> 59.5 us
  matrix products: 59.2 us -> 0 us
  other arithmetic: 50.1 us -> 1.65 us
  starting transfers between devices: 34 us -> 0 us
  between operations: 15.1 us -> 0.68 us
  loops' own time: 11.3 us -> 0 us
    psum x4 -> x0, waiting for transfers between devices: 143 us -> none  [over_axes(): return functools.reduce(lax.psum, axes, array)]
    gather x42 -> x0, local copies, waits for them, and re-layouts: 86.4 us -> none  [the longest x6 49.1 us: fold_banded(): jnp.diagonal(blocks, offset=1 - lift_index, axis1=1, axis2=3)]
    pallas_call x0 -> x1, Pallas kernels: none -> 59.5 us  [run(): pl.pallas_call(functools.partial(block_kernel, n_gx, n_gy), out_shape=(ja...]
    dot_general x54 -> x0, matrix products: 59.2 us -> none  [the longest x18 25.3 us: adjoint_conv(): lax.dot_general(window.reshape(-1, width), banded[offset], (((1,), (1,)),...]
    another operation x25 -> x8, local copies, waits for them, and re-layouts: 51.8 us -> 0.34 us  [the longest x4 0.33 us: run(): jnp.stack([jnp.tile(v, 4) for v in (scale_one, shift_one, scale_two, shif...]
    squeeze x18 -> x0, local copies, waits for them, and re-layouts: 43.2 us -> none  [forward_conv(): running = running + flat_dot(window, banded[offset])]
    unnamed x153 -> x22, local copies, waits for them, and re-layouts: 49.4 us -> 8.67 us
    ppermute x12 -> x0, starting transfers between devices: 33.8 us -> none  [the longest x4 16 us: extended(): before = lax.ppermute(last, axis, up)]
  transfers between devices with their start and end apart: 16 -> 0, of which waited for: 6 -> 0; matrix products, arithmetic and copies ran while one was open for 24% -> 0% of each run, Pallas kernels for 0% -> 0%
where the time goes in v1:
time: 71.2 us; the launch traced here: 70.9 us
  Pallas kernels  59.5 us (84%)
  local copies, waits for them, and re-layouts  9.01 us (13%)
  other arithmetic  1.65 us (2%)
    pallas_call x1, Pallas kernels, run(): pl.pallas_call(functools.partial(block_kernel, n_gx, n_gy), out_shape=(ja...  59.5 us
    unnamed x22, local copies, waits for them, and re-layouts  8.67 us

profile of v1, /device:TPU:1, one launch (start us, length us, event | category | flops | bytes accessed | tf_op | source)
XLA Modules:
  0.0 70.9 jit_solution(490764954802733424)
XLA Ops:
  0.6 0.0 copy-start.5
  0.7 0.6 copy-done.5
  1.3 0.0 copy-start.6
  1.3 0.1 stack_tile.12
  1.4 0.6 copy-done.6
  1.9 0.0 copy-start.7
  1.9 0.1 stack_tile.13
  2.0 0.6 copy-done.7
  2.6 0.0 copy-start.8
  2.6 0.0 copy-start.3
  2.6 0.0 copy-start.4
  2.6 0.1 stack_tile.14
  2.7 0.6 copy-done.8
  3.3 0.1 stack_tile.15
  3.3 0.6 pad_maximum_fusion.par
  3.9 0.0 copy-done.3
  4.0 0.0 copy-done.4
  4.0 1.0 %select_convert_fusion.bounds = bf16[16,64,128]{2,1,0:T(8,128)(2,1)} fusion(s32[16,64]{1,0:T(8,128)S(1)} %copy-done.3, s32[16,64]{1,0:T(8,128)S(1)} %copy-done.4, pred[128]{0:T(512)(128)(4,1)S(1)} %iota_compare_fusion), kind=kLoop, calls=%fused_computation | loop fusion | flops 262144 | bytes 270464 | tf_op jit(solution)/shard_map/convert_element_type | solution.py:644
  5.0 59.5 %residual_block.1 = (bf16[16,64,512]{2,1,0:T(8,128)(2,1)}, bf16[16,64,512]{2,1,0:T(8,128)(2,1)}, f32[1728,64]{1,0:T(8,128)}, f32[1728,64]{1,0:T(8,128)}) custom-call(bf16[16,64,512]{2,1,0:T(8,128)(2,1)} %feat.1, bf16[16,64,128]{2,1,0:T(8,128)(2,1)} %select_convert_fusion.bounds, bf16[16,64,512]{2,1,0:T(8,128)(2,1)} %cot.1, s32[16,64]{1,0:T(8,128)} %low.1, ...), custom_call_target="tpu_custom_call" | custom-call | tf_op jit(solution)/shard_map/residual_block/pallas_call | solution.py:703
  64.5 0.0 copy-start
  64.6 2.4 %copy.18 = bf16[16,64,512]{2,1,0:T(8,128)(2,1)} copy(bf16[16,64,512]{2,1,0:T(8,128)(2,1)} %get-tuple-element.16) | data formatting | bytes 2097152
  66.9 0.0 copy-done
  66.9 0.0 copy-start.2
  66.9 1.0 %copy.19 = bf16[16,64,512]{2,1,0:T(8,128)(2,1)} copy(bf16[16,64,512]{2,1,0:T(8,128)(2,1)S(1)} %copy-done) | data formatting | bytes 2097152
  67.9 0.6 copy-done.2
  68.5 0.0 copy-start.1
  68.5 0.9 %copy.20 = f32[27,64,64]{2,1,0:T(8,128)} copy(f32[27,64,64]{2,1,0:T(8,128)S(1)} %bitcast.5) | data formatting | bytes 884736
  69.4 0.6 copy-done.1
  70.0 0.9 %copy.21 = f32[27,64,64]{2,1,0:T(8,128)} copy(f32[27,64,64]{2,1,0:T(8,128)S(1)} %bitcast.4) | data formatting | bytes 884736
  (5 shorter events, 0.0 us)
Async XLA Ops:
  0.6 0.7 copy-start.5
  1.3 0.7 copy-start.6
  1.9 0.7 copy-start.7
  2.6 0.7 copy-start.8
  2.6 1.3 %copy-start.3 = (s32[16,64]{1,0:T(8,128)S(1)}, s32[16,64]{1,0:T(8,128)}, u32[]{:S(2)}) copy-start(s32[16,64]{1,0:T(8,128)} %high.1) | copy-start | bytes 12292
  2.6 1.3 %copy-start.4 = (s32[16,64]{1,0:T(8,128)S(1)}, s32[16,64]{1,0:T(8,128)}, u32[]{:S(2)}) copy-start(s32[16,64]{1,0:T(8,128)} %low.1) | copy-start | bytes 12292
  64.5 2.4 %copy-start = (bf16[16,64,512]{2,1,0:T(8,128)(2,1)S(1)}, bf16[16,64,512]{2,1,0:T(8,128)(2,1)}, u32[]{:S(2)}) copy-start(bf16[16,64,512]{2,1,0:T(8,128)(2,1)} %get-tuple-element.17) | copy-start | bytes 3145732
  66.9 1.5 %copy-start.2 = (f32[1728,64]{1,0:T(8,128)S(1)}, f32[1728,64]{1,0:T(8,128)}, u32[]{:S(2)}) copy-start(f32[1728,64]{1,0:T(8,128)} %get-tuple-element.10) | copy-start | bytes 1327108
  68.5 1.5 %copy-start.1 = (f32[1728,64]{1,0:T(8,128)S(1)}, f32[1728,64]{1,0:T(8,128)}, u32[]{:S(2)}) copy-start(f32[1728,64]{1,0:T(8,128)} %get-tuple-element.11) | copy-start | bytes 1327108

commit v2 on v1

--- a/solution.py
+++ b/solution.py
@@ -151,17 +151,25 @@
     n_gx,
     n_gy,
     feat,
-    bounds,
+    cot_in,
+    w_one_in,
+    w_two_in,
+    low_in,
+    high_in,
+    scale_one_in,
+    shift_one_in,
+    scale_two_in,
+    shift_two_in,
+    out,
+    gfeat,
+    full,
     cot,
+    w_one,
+    w_two,
     low,
     high,
-    w_one,
-    w_two,
-    par,
-    out,
-    gfeat,
-    gw_one,
-    gw_two,
+    scales,
+    bounds,
     ext,
     elh,
     pick_in,
@@ -191,7 +199,6 @@
     got_x,
     half,
     got_y,
-    full,
     out_x,
     in_x,
     out_y,
@@ -214,6 +221,13 @@
     nx, ny = feat.shape[0], feat.shape[1]
     per = BLOCKS // n_gx
 
+    inputs = [
+        pltpu.make_async_copy(src, dst, local_sem.at[2 + k])
+        for k, (src, dst) in enumerate(
+            ((w_one_in, w_one), (w_two_in, w_two), (cot_in, cot))
+        )
+    ]
+
     def device(dx, dy):
         return (lax.rem(gx + dx + n_gx, n_gx), lax.rem(gy + dy + n_gy, n_gy))
 
@@ -225,6 +239,38 @@
             pl.semaphore_signal(
                 barrier, inc=1, device_id=device(dx, dy), device_id_type=MESH
             )
+
+    own = pltpu.make_async_copy(
+        feat, ext.at[2 : nx + 2, 16 : ny + 16], local_sem.at[0]
+    )
+    own.start()
+    small = [
+        pltpu.make_async_copy(src, dst, local_sem.at[5 + k])
+        for k, (src, dst) in enumerate(
+            (
+                (low_in, low),
+                (high_in, high),
+                (scale_one_in, scales.at[0]),
+                (shift_one_in, scales.at[1]),
+                (scale_two_in, scales.at[2]),
+                (shift_two_in, scales.at[3]),
+            )
+        )
+    ]
+    for copy in small + inputs:
+        copy.start()
+    for copy in small:
+        copy.wait()
+
+    first = lane((ny, 128)) < 64
+    square = jnp.zeros((ny, ny), F32)
+    lows = jnp.concatenate([low[...].astype(F32), square[nx:]], axis=0).T
+    highs = jnp.concatenate([high[...].astype(F32), square[nx:]], axis=0).T
+    for x in range(nx):
+        both = jnp.where(first, lows[:, x : x + 1], highs[:, x : x + 1]).astype(BF16)
+        bounds[x] = both
+        elh[x + 2, 16 : ny + 16, :] = both
+    if comm:
         pl.semaphore_wait(barrier, len(peers))
 
     def remote(src, dst, send, recv, to):
@@ -255,16 +301,9 @@
                 )
                 copy.start()
                 halos.append(copy)
-    own = [
-        pltpu.make_async_copy(
-            src, dst.at[2 : nx + 2, 16 : ny + 16], local_sem.at[k]
-        )
-        for k, (src, dst) in enumerate(((feat, ext), (bounds, elh)))
-    ]
-    for copy in own:
-        copy.start()
-
+    inputs[0].wait()
     build_weights(w_one, fwd_one, adj_one)
+    inputs[1].wait()
     build_weights(w_two, fwd_two, adj_two)
     nothing = jnp.zeros((3, 2 * ROWS, WIDTH), BF16)
     err_two[:, 0 : 2 * ROWS, :] = nothing
@@ -309,32 +348,28 @@
     put_out[...] = picks(CORE, 2 * ny, 1, BRICK, ny, 0)
     put_grad[...] = picks(ROWS, 2 * (ny + 16), 1, W, ny + 16, 6)
 
+    inputs[2].wait()
     def cut_target(x, carry):
         rows = jnp.concatenate([cot[x], cot[8 + x]], axis=0)
         spot = pl.ds(pl.multiple_of(x * CORE, CORE), CORE)
         target[spot, :] = jnp.dot(pick_target[...], rows, preferred_element_type=F32)
         return carry
 
-    lax.fori_loop(0, 8, cut_target, 0)
-
-    def mask_in(x, y0, n):
-        mask = height_mask(elh[x, y0 : y0 + n, :].astype(F32))
+    lax.fori_loop(0, 8, cut_target, 0, unroll=8)
+
+    def mask_in(xs, ys):
+        mask = height_mask(elh[xs, ys, :].astype(F32))
         for c in range(4):
             lanes = slice(128 * c, 128 * c + 128)
-            value = ext[x, y0 : y0 + n, lanes].astype(F32)
-            ext[x, y0 : y0 + n, lanes] = jnp.where(mask[c], value, 0.0).astype(BF16)
-
-    def mask_rows(*spots):
-        def one(x, carry):
-            for y0, n in spots:
-                mask_in(x, y0, n)
-            return carry
-
-        return one
-
-    for copy in own:
-        copy.wait()
-    lax.fori_loop(2, nx + 2, mask_rows((16, ny)), 0)
+            value = ext[xs, ys, lanes].astype(F32)
+            ext[xs, ys, lanes] = jnp.where(mask[c], value, 0.0).astype(BF16)
+
+    def mask_inner(i, carry):
+        mask_in(pl.ds(2 + 2 * i, 2), slice(16, ny + 16))
+        return carry
+
+    own.wait()
+    lax.fori_loop(0, nx // 2, mask_inner, 0, unroll=2)
     for copy in halos:
         copy.wait()
     if comm:
@@ -356,9 +391,11 @@
             elh[:, spot] = jnp.zeros_like(elh[:, spot])
             ext[:, spot] = jnp.zeros_like(ext[:, spot])
 
-    lax.fori_loop(2, nx + 2, mask_rows((0, 16), (ny + 16, 16)), 0)
-    for x in (0, nx + 2):
-        lax.fori_loop(x, x + 2, mask_rows((0, tall)), 0)
+    for x in range(2, nx + 2, 4):
+        mask_in(slice(x, x + 4), slice(0, 16))
+        mask_in(slice(x, x + 4), slice(ny + 16, tall))
+    for x in (0, 1, nx + 2, nx + 3):
+        mask_in(slice(x, x + 1), slice(0, tall))
 
     def cut(x, carry):
         base = pl.multiple_of(x * ROWS, ROWS)
@@ -381,10 +418,11 @@
             core_mask[pl.ds(core, CORE), lanes] = value[ROWS:]
         return carry
 
-    lax.fori_loop(0, W, cut, 0)
-
-    scale_one, shift_one = par[0:1, :], par[1:2, :]
-    scale_two, shift_two = par[2:3, :], par[3:4, :]
+    lax.fori_loop(0, W, cut, 0, unroll=4)
+
+    scale_one, shift_one, scale_two, shift_two = (
+        jnp.concatenate([scales[k]] * 4, axis=1) for k in range(4)
+    )
 
     for g in range(2):
         lanes = slice(256 * g, 256 * g + 256)
@@ -429,7 +467,7 @@
                 err_two[oy, pl.ds(base, ROWS), lanes] = moved.astype(BF16)
         return carry
 
-    lax.fori_loop(0, 8, spread, 0)
+    lax.fori_loop(0, 8, spread, 0, unroll=2)
 
     def exchange(conv_id):
         copies = []
@@ -535,7 +573,7 @@
             gsum[x] = total
             return carry
 
-        lax.fori_loop(start, stop, collect, 0)
+        lax.fori_loop(start, stop, collect, 0, unroll=4)
 
     edges = []
     if comm:
@@ -569,7 +607,7 @@
         out[8 + x] = value[ny:]
         return carry
 
-    lax.fori_loop(0, 8, deposit, 0)
+    lax.fori_loop(0, 8, deposit, 0, unroll=4)
 
     add_up(0, sent_one_y, got_y, half.at[1], n_gy)
     sent_one_full = gather(0)
@@ -605,12 +643,11 @@
             gfeat[x, :, lanes] = jnp.where(mask[c], value, 0.0).astype(BF16)
         return carry
 
-    lax.fori_loop(0, nx, finish, 0)
-
-    for conv_id, copies, gw in ((1, sent_two_full, gw_two), (0, sent_one_full, gw_one)):
+    lax.fori_loop(0, nx, finish, 0, unroll=4)
+
+    for copies in (sent_two_full, sent_one_full):
         for copy in copies:
             copy.wait_recv()
-        unfold(full.at[conv_id], per, gw, 1.0 / (n_gx * n_gy * SHARE))
     for copies in (
         edges,
         sent_one,
@@ -622,6 +659,24 @@
     ):
         for copy in copies:
             copy.wait_send()
+
+
+def result_kernel(
+    factor, per, out_in, gfeat_in, full, out, gfeat, gw_one, gw_two, one, two, sem
+):
+    copies = [
+        pltpu.make_async_copy(out_in, out, sem.at[0]),
+        pltpu.make_async_copy(gfeat_in, gfeat, sem.at[1]),
+    ]
+    for copy in copies:
+        copy.start()
+    for k, (ref, gw) in enumerate(((one, gw_one), (two, gw_two))):
+        unfold(full.at[k], per, ref, factor)
+        copy = pltpu.make_async_copy(ref, gw, sem.at[2 + k])
+        copy.start()
+        copies.append(copy)
+    for copy in copies:
+        copy.wait()
 
 
 def run(
@@ -640,16 +695,18 @@
 ):
     nx, ny = features.shape[0], features.shape[1]
     per = BLOCKS // n_gx
-    first = lax.broadcasted_iota(jnp.int32, (nx, ny, 128), 2) < 64
-    bounds = jnp.where(first, low[..., None], high[..., None]).astype(BF16)
-    par = jnp.stack(
-        [jnp.tile(v, 4) for v in (scale_one, shift_one, scale_two, shift_two)]
-    )
     whole = pl.BlockSpec(memory_space=pltpu.VMEM)
     left = pl.BlockSpec(memory_space=pl.ANY)
     vm = pltpu.VMEM
     dma = pltpu.SemaphoreType.DMA
     scratch = [
+        vm((nx, ny, WIDTH), BF16),
+        vm((27 * C, C), BF16),
+        vm((27 * C, C), BF16),
+        vm((nx, ny), jnp.int32),
+        vm((nx, ny), jnp.int32),
+        vm((4, 1, C), F32),
+        vm((nx, ny, 128), BF16),
         vm((nx + 4, ny + 32, WIDTH), BF16),
         vm((nx + 4, ny + 32, 128), BF16),
         vm((3 * ROWS + CORE, 2 * ny + 64), BF16),
@@ -679,14 +736,13 @@
         vm((2, n_gx, per, 64, 128), BF16),
         vm((2, 2, per, 64, 128), BF16),
         vm((2, n_gy, per, 64, 128), BF16),
-        vm((2, n_gx, per, 64, 128), BF16),
         vm((2, 2, ny, WIDTH), BF16),
         vm((2, 2, ny, WIDTH), BF16),
         vm((2, nx // 2, 16, WIDTH), BF16),
         vm((2, nx // 2, 16, WIDTH), BF16),
         vm((2, 2, 16, WIDTH), BF16),
         vm((2, 2, 16, WIDTH), BF16),
-        dma((2,)),
+        dma((11,)),
         dma((2, 8)),
         dma((2, 8)),
         dma((8,)),
@@ -698,31 +754,46 @@
     params = pltpu.CompilerParams(
         collective_id=0 if comm else None,
         has_side_effects=comm,
-        vmem_limit_bytes=60 * 2**20,
+        vmem_limit_bytes=46 * 2**20,
     )
-    out, gfeat, gw_one, gw_two = pl.pallas_call(
+    in_hbm = functools.partial(
+        pltpu.with_memory_space_constraint, memory_space=pltpu.HBM
+    )
+    columns = jax.ShapeDtypeStruct(features.shape, BF16)
+    out, gfeat, full = pl.pallas_call(
         functools.partial(block_kernel, n_gx, n_gy),
         out_shape=(
-            jax.ShapeDtypeStruct(features.shape, BF16),
-            jax.ShapeDtypeStruct(features.shape, BF16),
-            jax.ShapeDtypeStruct((27 * C, C), F32),
-            jax.ShapeDtypeStruct((27 * C, C), F32),
+            columns,
+            columns,
+            jax.ShapeDtypeStruct((2, n_gx, per, 64, 128), BF16),
         ),
-        in_specs=[left, left] + [whole] * 6,
-        out_specs=(whole,) * 4,
+        in_specs=[pl.BlockSpec(memory_space=pltpu.HBM)] * 10,
+        out_specs=(whole,) * 3,
         scratch_shapes=scratch,
         compiler_params=params,
         name="residual_block",
     )(
-        features,
-        bounds,
-        cotangent,
-        low,
-        high,
-        weight_one.reshape(27 * C, C),
-        weight_two.reshape(27 * C, C),
-        par,
+        in_hbm(features),
+        in_hbm(cotangent),
+        in_hbm(weight_one.reshape(27 * C, C)),
+        in_hbm(weight_two.reshape(27 * C, C)),
+        in_hbm(low),
+        in_hbm(high),
+        in_hbm(scale_one.reshape(1, C)),
+        in_hbm(shift_one.reshape(1, C)),
+        in_hbm(scale_two.reshape(1, C)),
+        in_hbm(shift_two.reshape(1, C)),
     )
+    sums = jax.ShapeDtypeStruct((27 * C, C), F32)
+    out, gfeat, gw_one, gw_two = pl.pallas_call(
+        functools.partial(result_kernel, 1.0 / (n_gx * n_gy * SHARE), per),
+        out_shape=(columns, columns, sums, sums),
+        in_specs=[left, left, whole],
+        out_specs=(left,) * 4,
+        scratch_shapes=[vm((27 * C, C), F32), vm((27 * C, C), F32), dma((4,))],
+        compiler_params=pltpu.CompilerParams(vmem_limit_bytes=8 * 2**20),
+        name="results",
+    )(out, gfeat, full)
     return out, gfeat, gw_one.reshape(27, C, C), gw_two.reshape(27, C, C)
 
 

time: 71.2 us -> 53.8 us (0.76)
  local copies, waits for them, and re-layouts: 9.01 us -> 0 us
  Pallas kernels: 59.5 us -> 53 us
  other arithmetic: 1.65 us -> 0 us
    unnamed x22 -> x0, local copies, waits for them, and re-layouts: 8.67 us -> none
    pallas_call x1 -> x2, Pallas kernels: 59.5 us -> 53 us  [the longest x1 51.1 us: run(): pl.pallas_call(functools.partial(block_kernel, n_gx, n_gy), out_shape=(co...]
    convert_element_type x1 -> x0, other arithmetic: 1.04 us -> none  [run(): bounds = jnp.where(first, low[..., None], high[..., None]).astype(BF16)]
where the time goes in v2:
time: 53.8 us; the launch traced here: 53.7 us
  Pallas kernels  53 us (99%)
  between operations  0.64 us (1%)
    pallas_call x1, Pallas kernels, run(): pl.pallas_call(functools.partial(block_kernel, n_gx, n_gy), out_shape=(co...  51.1 us
    pallas_call x1, Pallas kernels, run(): pl.pallas_call(functools.partial(result_kernel, 1.0 / (n_gx * n_gy * SHAR...  1.93 us

profile of v2, /device:TPU:1, one launch (start us, length us, event | category | flops | bytes accessed | tf_op | source)
XLA Modules:
  0.0 53.7 jit_solution(15597845585637415204)
XLA Ops:
  0.6 51.1 %residual_block.1 = (bf16[16,64,512]{2,1,0:T(8,128)(2,1)S(1)}, bf16[16,64,512]{2,1,0:T(8,128)(2,1)S(1)}, bf16[2,16,1,64,128]{4,3,2,1,0:T(8,128)(2,1)S(1)}) custom-call(bf16[16,64,512]{2,1,0:T(8,128)(2,1)} %feat.1, bf16[16,64,512]{2,1,0:T(8,128)(2,1)} %cot_in.1, bf16[1728,64]{1,0:T(8,128)(2,1)} %bitcast.8, bf16[1728,64]{1,0:T(8,128)(2,1)} %bitcast.9, ...), custom_call_target="tpu_custom_call" | custom-call | tf_op jit(solution)/shard_map/residual_block/pallas_call | solution.py:763
  51.7 1.9 %results.1 = (bf16[16,64,512]{2,1,0:T(8,128)(2,1)}, bf16[16,64,512]{2,1,0:T(8,128)(2,1)}, f32[1728,64]{1,0:T(8,128)}, f32[1728,64]{1,0:T(8,128)}) custom-call(bf16[16,64,512]{2,1,0:T(8,128)(2,1)S(1)} %get-tuple-element.11.out_in, bf16[16,64,512]{2,1,0:T(8,128)(2,1)S(1)} %get-tuple-element.12.gfeat_in, bf16[2,16,1,64,128]{4,3,2,1,0:T(8,128)(2,1)S(1)} %get-tuple-element.13.full), custom_call_target="tpu_custom_call" | custom-call | tf_op jit(solution)/shard_map/results/pallas_call | solution.py:788

commit v3 on v2

--- a/solution.py
+++ b/solution.py
@@ -20,6 +20,7 @@
 ROWS = SLOTS * W
 CORE = SLOTS * BRICK
 BLOCKS = 16
+USED = 14
 HALOS = [(dx, dy) for dx in (-1, 0, 1) for dy in (-1, 0, 1) if dx or dy]
 
 
@@ -41,19 +42,17 @@
 
 def toeplitz(one, two, pair_ref, t):
     first = lane(one.shape) < 64
-    zero = jnp.zeros_like(one)
-    start = jnp.where(first, turned(one), zero)
-    end = jnp.where(first, zero, turned(two))
-    whole = [zero, start, one, two, end, zero]
+    zero = jnp.zeros(one.shape, BF16)
+    start = jnp.where(first, turned(one), 0.0).astype(BF16)
+    end = jnp.where(first, 0.0, turned(two)).astype(BF16)
+    one, two = one.astype(BF16), two.astype(BF16)
+    rows = pl.ds(pl.multiple_of(t * 512, 512), 512)
     columns = (
-        ([one, two, end, zero, zero, zero], whole),
-        (whole, [zero, zero, zero, start, one, two]),
-    )
-    rows = pl.ds(pl.multiple_of(t * 384, 384), 384)
-    for g in range(2):
-        for c in range(2):
-            block = jnp.concatenate(columns[g][c], axis=0).astype(BF16)
-            pair_ref[g, rows, 128 * c : 128 * c + 128] = block
+        [zero, start, one, two, end, zero, zero, zero],
+        [zero, zero, zero, start, one, two, end, zero],
+    )
+    for c in range(2):
+        pair_ref[rows, 128 * c : 128 * c + 128] = jnp.concatenate(columns[c], axis=0)
 
 
 def build_weights(w_ref, forward_ref, adjoint_ref):
@@ -72,16 +71,25 @@
     lax.fori_loop(0, 9, tap, 0)
 
 
-def conv(source, pair_ref, g, start, count, pitch):
+def conv(source, band_ref, g, spans, pitch):
     lanes = slice(128 * g, 128 * g + 384)
     parts = [
-        source[oy, start + ox * pitch : start + ox * pitch + count, lanes]
-        for ox in range(3)
-        for oy in range(3)
+        jnp.concatenate(
+            [
+                source[oy, start + ox * pitch : start + ox * pitch + count, lanes]
+                for ox in range(3)
+                for oy in range(3)
+            ],
+            axis=1,
+        )
+        for start, count in spans
     ]
-    return jnp.dot(
-        jnp.concatenate(parts, axis=1), pair_ref[g], preferred_element_type=F32
-    )
+    rows = parts[0] if len(parts) == 1 else jnp.concatenate(parts, axis=0)
+    skip = 128 * (1 - g)
+    band = jnp.concatenate(
+        [band_ref[512 * t + skip : 512 * t + skip + 384, :] for t in range(9)], axis=0
+    )
+    return jnp.dot(rows, band, preferred_element_type=F32)
 
 
 def shifted(value):
@@ -89,7 +97,7 @@
     return (pltpu.roll(value, 1, 0), value, pltpu.roll(value, count - 1, 0))
 
 
-def fold(results, fold_ref, t0):
+def fold(results, fold_ref, block_ref, t0):
     for oy in range(3):
         sums = {}
         for g in range(2):
@@ -105,13 +113,13 @@
                         sums[kind] = sums[kind] + block if kind in sums else block
         p, u, q, s = sums[0, 0], sums[0, -2], sums[1, -1], sums[1, 1]
         first = lane(p.shape) < 64
-        fold_ref[t0 + oy] = q + turned(jnp.where(first, p, u))
-        fold_ref[9 + t0 + oy] = p + turned(s)
-
-
-def weight_sums(errors_t, source, start, count, pitch, fold_ref, block_ref):
+        block_ref[t0 + oy] = (q + turned(jnp.where(first, p, u))).astype(BF16)
+        fold_ref[t0 + oy] = p + turned(s)
+
+
+def weight_sums(errors_t, source, count, pitch, fold_ref, block_ref, send):
     def column(ox, carry):
-        base = pl.multiple_of(start + ox * pitch, 16)
+        base = pl.multiple_of(ox * pitch, 16)
         results = []
         for g in range(2):
             lanes = slice(128 * g, 128 * g + 384)
@@ -121,19 +129,18 @@
             results.append(
                 jnp.dot(errors_t[g], window, preferred_element_type=F32)
             )
-        fold(results, fold_ref, 3 * ox)
+        fold(results, fold_ref, block_ref, 3 * ox)
+        for oy in range(3):
+            send(3 * ox + oy)
         return carry
 
     lax.fori_loop(0, 3, column, 0)
     first = lane((64, 128)) < 64
-    for t in range(9):
-        block_ref[t] = fold_ref[t].astype(BF16)
     for i in range(5):
-        even = turned(fold_ref[9 + 2 * i])
-        odd = fold_ref[10 + 2 * i] if i < 4 else jnp.zeros_like(even)
+        even = turned(fold_ref[2 * i])
+        odd = fold_ref[2 * i + 1] if i < 4 else jnp.zeros_like(even)
         block_ref[9 + i] = jnp.where(first, even, odd).astype(BF16)
-    block_ref[14] = jnp.zeros((64, 128), BF16)
-    block_ref[15] = jnp.zeros((64, 128), BF16)
+        send(9 + i)
 
 
 def unfold(blocks_ref, per, out_ref, factor):
@@ -201,6 +208,7 @@
     got_y,
     out_x,
     in_x,
+    edge_rows,
     out_y,
     in_y,
     out_c,
@@ -270,9 +278,6 @@
         both = jnp.where(first, lows[:, x : x + 1], highs[:, x : x + 1]).astype(BF16)
         bounds[x] = both
         elh[x + 2, 16 : ny + 16, :] = both
-    if comm:
-        pl.semaphore_wait(barrier, len(peers))
-
     def remote(src, dst, send, recv, to):
         return pltpu.make_async_remote_copy(
             src_ref=src,
@@ -283,6 +288,11 @@
             device_id_type=MESH,
         )
 
+    inputs[0].wait()
+    build_weights(w_one, fwd_one, adj_one)
+
+    if comm:
+        pl.semaphore_wait(barrier, len(peers))
     halos = []
     if comm:
         x_from = {-1: slice(0, 2), 0: slice(0, nx), 1: slice(nx - 2, nx)}
@@ -301,8 +311,6 @@
                 )
                 copy.start()
                 halos.append(copy)
-    inputs[0].wait()
-    build_weights(w_one, fwd_one, adj_one)
     inputs[1].wait()
     build_weights(w_two, fwd_two, adj_two)
     nothing = jnp.zeros((3, 2 * ROWS, WIDTH), BF16)
@@ -426,7 +434,7 @@
 
     for g in range(2):
         lanes = slice(256 * g, 256 * g + 256)
-        pre = conv(src_one, fwd_one, g, 0, 10 * ROWS, ROWS) * scale_one + shift_one
+        pre = conv(src_one, fwd_one, g, [(0, 10 * ROWS)], ROWS) * scale_one + shift_one
         s = jax.nn.sigmoid(pre)
         mask = msk[ROWS : 11 * ROWS, lanes]
         hidden = pre * s * mask
@@ -446,7 +454,7 @@
     errors_t = []
     for g in range(2):
         lanes = slice(256 * g, 256 * g + 256)
-        pre = conv(src_two, fwd_two, g, 0, 8 * CORE, CORE) * scale_two + shift_two
+        pre = conv(src_two, fwd_two, g, [(0, 8 * CORE)], CORE) * scale_two + shift_two
         pre = pre + core_in[middle, lanes]
         s = jax.nn.sigmoid(pre)
         mask = core_mask[middle, lanes]
@@ -469,70 +477,95 @@
 
     lax.fori_loop(0, 8, spread, 0, unroll=2)
 
-    def exchange(conv_id):
-        copies = []
-        for d in range(1, n_gx):
-            to = lax.rem(gx + d, n_gx)
-            copy = remote(
-                blocks.at[conv_id, pl.ds(to * per, per)],
-                got_x.at[conv_id, gx],
-                sum_send.at[conv_id, 0, d],
-                sum_recv.at[conv_id, 0, d],
-                (to, gy),
-            )
-            copy.start()
-            copies.append(copy)
-        got_x[conv_id, gx] = blocks[conv_id, pl.ds(gx * per, per)]
-        return copies
-
-    def add_up(conv_id, copies, source, where, n):
-        for copy in copies:
-            copy.wait_recv()
-        total = source[conv_id, 0].astype(F32)
-        for s in range(1, n):
-            total = total + source[conv_id, s].astype(F32)
-        where[conv_id] = total.astype(BF16)
-        return copies
-
-    def exchange_y(conv_id):
-        copies = []
-        for d in range(1, n_gy):
-            copy = remote(
-                half.at[0, conv_id],
-                got_y.at[conv_id, gy],
-                sum_send.at[conv_id, 1, d],
-                sum_recv.at[conv_id, 1, d],
-                (gx, lax.rem(gy + d, n_gy)),
-            )
-            copy.start()
-            copies.append(copy)
-        got_y[conv_id, gy] = half[0, conv_id]
-        return copies
-
-    def gather(conv_id):
-        copies = []
-        for d in range(1, n_gx):
-            copy = remote(
-                half.at[1, conv_id],
-                full.at[conv_id, gx],
-                sum_send.at[conv_id, 2, d],
-                sum_recv.at[conv_id, 2, d],
-                (lax.rem(gx + d, n_gx), gy),
-            )
-            copy.start()
-            copies.append(copy)
-        full[conv_id, gx] = half[1, conv_id]
-        return copies
+    def block_copy(conv_id, b, sender):
+        return remote(
+            blocks.at[conv_id, b],
+            got_x.at[conv_id, sender, 0],
+            sum_send.at[conv_id, 0, b],
+            sum_recv.at[conv_id, 0, sender],
+            (b, gy),
+        )
+
+    def sender_of(conv_id):
+        def send(b):
+            if not comm:
+                got_x[conv_id, 0, b] = blocks[conv_id, b]
+                return
+
+            @pl.when(gx != b)
+            def _():
+                block_copy(conv_id, b, gx).start()
+
+            @pl.when(gx == b)
+            def _():
+                got_x[conv_id, gx, 0] = blocks[conv_id, b]
+
+        return send
+
+    def y_copy(conv_id, d):
+        return remote(
+            half.at[0, conv_id],
+            got_y.at[conv_id, gy],
+            sum_send.at[conv_id, 1, d],
+            sum_recv.at[conv_id, 1, d],
+            (gx, lax.rem(gy + d, n_gy)),
+        )
+
+    def full_copy(conv_id, to, owner):
+        return remote(
+            half.at[1, conv_id],
+            full.at[conv_id, owner],
+            sum_send.at[conv_id, 2, to],
+            sum_recv.at[conv_id, 2, owner],
+            (to, gy),
+        )
+
+    def owners(act):
+        if comm:
+            pl.when(gx < USED)(act)
+        else:
+            act()
+
+    def others(n, act):
+        for k in range(n):
+            pl.when(gx != k)(functools.partial(act, k))
+
+    def reduce_x(conv_id):
+        def act():
+            if comm:
+                others(n_gx, lambda s: block_copy(conv_id, 0, s).wait_recv())
+            total = got_x[conv_id, 0].astype(F32)
+            for s in range(1, n_gx):
+                total = total + got_x[conv_id, s].astype(F32)
+            half[0, conv_id] = total.astype(BF16)
+            for d in range(1, n_gy):
+                y_copy(conv_id, d).start()
+            got_y[conv_id, gy] = half[0, conv_id]
+
+        owners(act)
+
+    def reduce_y(conv_id):
+        def act():
+            for d in range(1, n_gy):
+                y_copy(conv_id, d).wait_recv()
+            total = got_y[conv_id, 0].astype(F32)
+            for s in range(1, n_gy):
+                total = total + got_y[conv_id, s].astype(F32)
+            half[1, conv_id] = total.astype(BF16)
+            if comm:
+                others(n_gx, lambda to: full_copy(conv_id, to, gx).start())
+            full[conv_id, gx] = half[1, conv_id]
+
+        owners(act)
 
     weight_sums(
-        errors_t, src_two, 0, 8 * CORE, CORE, folded, blocks.at[1]
-    )
-    sent_two = exchange(1)
+        errors_t, src_two, 8 * CORE, CORE, folded, blocks.at[1], sender_of(1)
+    )
 
     errors_t = []
     for g in range(2):
         lanes = slice(256 * g, 256 * g + 256)
-        back = conv(err_two, adj_two, g, 0, 10 * ROWS, ROWS)
+        back = conv(err_two, adj_two, g, [(0, 10 * ROWS)], ROWS)
         error = back * slope[:, lanes]
         errors_t.append(error.T.astype(BF16))
         for x in range(10):
@@ -540,53 +573,44 @@
             spot = slice(ROWS * (x + 2), ROWS * (x + 3))
             for oy, moved in enumerate(shifted(rows)):
                 err_one[oy, spot, lanes] = moved.astype(BF16)
-    weight_sums(errors_t, src_one, 0, 10 * ROWS, ROWS, folded, blocks.at[0])
-    sent_one = exchange(0)
-    add_up(1, sent_two, got_x, half.at[0], n_gx)
-    sent_two_y = exchange_y(1)
-
-    for g in range(2):
+    weight_sums(
+        errors_t, src_one, 10 * ROWS, ROWS, folded, blocks.at[0], sender_of(0)
+    )
+    reduce_x(1)
+
+    def adjoint_one(g, columns):
         lanes = slice(256 * g, 256 * g + 256)
-        back = conv(err_one, adj_one, g, 0, 12 * ROWS, ROWS)
-        for x in range(W):
-            rows = back[ROWS * x : ROWS * x + ROWS]
-            if 2 <= x < 10:
-                rows = rows + frame[x - 2, :, lanes]
-            grad_region[x, :, lanes] = rows.astype(BF16)
-
-    add_up(0, sent_one, got_x, half.at[0], n_gx)
-    sent_one_y = exchange_y(0)
-    add_up(1, sent_two_y, got_y, half.at[1], n_gy)
-    sent_two_full = gather(1)
-
-    for bxs, start, stop in (((0,), 0, 8), ((0, 1), 8, W), ((1,), W, 20)):
-
-        def collect(x, carry, bxs=bxs):
-            total = None
-            for bx in bxs:
+        spans = [(ROWS * x, ROWS * n) for x, n in columns]
+        back = conv(err_one, adj_one, g, spans, ROWS)
+        done = 0
+        for start, n in columns:
+            for x in range(start, start + n):
+                rows = back[ROWS * done : ROWS * done + ROWS]
+                if 2 <= x < 10:
+                    rows = rows + frame[x - 2, :, lanes]
+                grad_region[x, :, lanes] = rows.astype(BF16)
+                done += 1
+
+    def collect(x):
+        total = None
+        for bx in range(BX):
+            if 0 <= x - 8 * bx < W:
                 part = jnp.dot(
                     put_grad[bx * (ny + 16) : (bx + 1) * (ny + 16), :],
                     grad_region[x - 8 * bx],
                     preferred_element_type=F32,
                 )
                 total = part if total is None else total + part
-            gsum[x] = total
-            return carry
-
-        lax.fori_loop(start, stop, collect, 0, unroll=4)
-
+        return total
+
+    for g in range(2):
+        adjoint_one(g, [(0, 2), (10, 2)])
     edges = []
-    if comm:
-        out_x[0] = gsum[0:2, 8 : ny + 8, :].astype(BF16)
-        out_x[1] = gsum[nx + 2 : nx + 4, 8 : ny + 8, :].astype(BF16)
-        for side, t in enumerate((0, ny + 8)):
-            for i in range(nx // 2):
-                both = [gsum[2 + 2 * i + k, t : t + 8, :] for k in range(2)]
-                out_y[side, i] = jnp.concatenate(both, axis=0).astype(BF16)
-            for up, x in enumerate((0, nx + 2)):
-                both = [gsum[x + k, t : t + 8, :] for k in range(2)]
-                out_c[up, side] = jnp.concatenate(both, axis=0).astype(BF16)
+
+    def send_edges(kinds):
         for i, (dx, dy) in enumerate(HALOS):
+            if (dx, dy) not in kinds:
+                continue
             a, b = (dx + 1) // 2, (dy + 1) // 2
             if dy == 0:
                 src, dst = out_x.at[a], in_x.at[1 - a]
@@ -600,6 +624,33 @@
             copy.start()
             edges.append(copy)
 
+    if comm:
+        for a, x in enumerate((0, nx + 2)):
+            pair = [collect(x + k) for k in range(2)]
+            for k in range(2):
+                out_x[a, k] = pair[k][8 : ny + 8].astype(BF16)
+            for b, t in enumerate((0, ny + 8)):
+                both = [value[t : t + 8] for value in pair]
+                out_c[a, b] = jnp.concatenate(both, axis=0).astype(BF16)
+        send_edges([h for h in HALOS if h[0]])
+
+    adjoint_one(0, [(2, 8)])
+    reduce_x(0)
+    adjoint_one(1, [(2, 8)])
+    reduce_y(1)
+
+    for x in range(2, nx + 2):
+        value = collect(x)
+        gsum[x] = value
+        if comm:
+            rows = slice(2 * (x - 2), 2 * (x - 2) + 2)
+            edge_rows[0, rows, :] = value[6:8]
+            edge_rows[1, rows, :] = value[ny + 8 : ny + 10]
+    if comm:
+        out_y[...] = edge_rows[...].astype(BF16)
+        send_edges([h for h in HALOS if not h[0]])
+    reduce_y(0)
+
     def deposit(x, carry):
         rows = res[pl.ds(pl.multiple_of(x * CORE, CORE), CORE), :]
         value = jnp.dot(put_out[...], rows, preferred_element_type=F32).astype(BF16)
@@ -608,9 +659,6 @@
         return carry
 
     lax.fori_loop(0, 8, deposit, 0, unroll=4)
-
-    add_up(0, sent_one_y, got_y, half.at[1], n_gy)
-    sent_one_full = gather(0)
 
     if comm:
         for copy in edges:
@@ -629,11 +677,10 @@
                 rows = in_c[a, b].astype(F32) * (x_in[a] * y_in[b])
                 for k in range(2):
                     gsum[x + k, t : t + 8, :] += rows[8 * k : 8 * k + 8]
-        for b, t in enumerate((8, ny)):
-            for i in range(nx // 2):
-                rows = in_y[b, i].astype(F32) * y_in[b]
-                for k in range(2):
-                    gsum[2 + 2 * i + k, t : t + 8, :] += rows[8 * k : 8 * k + 8]
+        for b, t in enumerate((8, ny + 6)):
+            rows = in_y[b].astype(F32) * y_in[b]
+            for i in range(nx):
+                gsum[2 + i, t : t + 2, :] += rows[2 * i : 2 * i + 2]
 
     def finish(x, carry):
         mask = height_mask(elh[x + 2, 16 : ny + 16, :].astype(F32))
@@ -645,20 +692,20 @@
 
     lax.fori_loop(0, nx, finish, 0, unroll=4)
 
-    for copies in (sent_two_full, sent_one_full):
-        for copy in copies:
-            copy.wait_recv()
-    for copies in (
-        edges,
-        sent_one,
-        sent_two,
-        sent_one_y,
-        sent_two_y,
-        sent_one_full,
-        sent_two_full,
-    ):
-        for copy in copies:
+    if comm:
+        for conv_id in (1, 0):
+            others(USED, lambda k: full_copy(conv_id, 0, k).wait_recv())
+        for copy in edges:
             copy.wait_send()
+        for conv_id in (1, 0):
+            others(USED, lambda b: block_copy(conv_id, b, gx).wait_send())
+
+            def sent(conv_id=conv_id):
+                for d in range(1, n_gy):
+                    y_copy(conv_id, d).wait_send()
+                others(n_gx, lambda to: full_copy(conv_id, to, gx).wait_send())
+
+            owners(sent)
 
 
 def result_kernel(
@@ -727,19 +774,20 @@
         vm((8 * CORE, WIDTH), BF16),
         vm((W, ROWS, WIDTH), BF16),
         vm((nx + 4, ny + 16, WIDTH), F32),
-        vm((2, 27 * 128, 256), BF16),
-        vm((2, 27 * 128, 256), BF16),
-        vm((2, 27 * 128, 256), BF16),
-        vm((2, 27 * 128, 256), BF16),
-        vm((18, 64, 128), F32),
+        vm((9 * 512, 256), BF16),
+        vm((9 * 512, 256), BF16),
+        vm((9 * 512, 256), BF16),
+        vm((9 * 512, 256), BF16),
+        vm((9, 64, 128), F32),
         vm((2, BLOCKS, 64, 128), BF16),
         vm((2, n_gx, per, 64, 128), BF16),
         vm((2, 2, per, 64, 128), BF16),
         vm((2, n_gy, per, 64, 128), BF16),
         vm((2, 2, ny, WIDTH), BF16),
         vm((2, 2, ny, WIDTH), BF16),
-        vm((2, nx // 2, 16, WIDTH), BF16),
-        vm((2, nx // 2, 16, WIDTH), BF16),
+        vm((2, 2 * nx, WIDTH), F32),
+        vm((2, 2 * nx, WIDTH), BF16),
+        vm((2, 2 * nx, WIDTH), BF16),
         vm((2, 2, 16, WIDTH), BF16),
         vm((2, 2, 16, WIDTH), BF16),
         dma((11,)),

time: 53.8 us -> 51.2 us (0.952)
  Pallas kernels: 53 us -> 50.4 us
    pallas_call x1, Pallas kernels: 51.1 us -> 48.4 us  [run(): pl.pallas_call(functools.partial(block_kernel, n_gx, n_gy), out_shape=(co...]
where the time goes in v3:
time: 51.2 us; the launch traced here: 51 us
  Pallas kernels  50.4 us (98%)
  between operations  0.64 us (1%)
    pallas_call x1, Pallas kernels, run(): pl.pallas_call(functools.partial(block_kernel, n_gx, n_gy), out_shape=(co...  48.4 us
    pallas_call x1, Pallas kernels, run(): pl.pallas_call(functools.partial(result_kernel, 1.0 / (n_gx * n_gy * SHAR...  1.93 us

profile of v3, /device:TPU:1, one launch (start us, length us, event | category | flops | bytes accessed | tf_op | source)
XLA Modules:
  0.0 51.0 jit_solution(6023043603131392241)
XLA Ops:
  0.6 48.4 %residual_block.1 = (bf16[16,64,512]{2,1,0:T(8,128)(2,1)S(1)}, bf16[16,64,512]{2,1,0:T(8,128)(2,1)S(1)}, bf16[2,16,1,64,128]{4,3,2,1,0:T(8,128)(2,1)S(1)}) custom-call(bf16[16,64,512]{2,1,0:T(8,128)(2,1)} %feat.1, bf16[16,64,512]{2,1,0:T(8,128)(2,1)} %cot_in.1, bf16[1728,64]{1,0:T(8,128)(2,1)} %bitcast.8, bf16[1728,64]{1,0:T(8,128)(2,1)} %bitcast.9, ...), custom_call_target="tpu_custom_call" | custom-call | tf_op jit(solution)/shard_map/residual_block/pallas_call | solution.py:811
  49.1 1.9 %results.1 = (bf16[16,64,512]{2,1,0:T(8,128)(2,1)}, bf16[16,64,512]{2,1,0:T(8,128)(2,1)}, f32[1728,64]{1,0:T(8,128)}, f32[1728,64]{1,0:T(8,128)}) custom-call(bf16[16,64,512]{2,1,0:T(8,128)(2,1)S(1)} %get-tuple-element.11.out_in, bf16[16,64,512]{2,1,0:T(8,128)(2,1)S(1)} %get-tuple-element.12.gfeat_in, bf16[2,16,1,64,128]{4,3,2,1,0:T(8,128)(2,1)S(1)} %get-tuple-element.13.full), custom_call_target="tpu_custom_call" | custom-call | tf_op jit(solution)/shard_map/results/pallas_call | solution.py:836

commit v4 on v3

--- a/solution.py
+++ b/solution.py
@@ -97,7 +97,7 @@
     return (pltpu.roll(value, 1, 0), value, pltpu.roll(value, count - 1, 0))
 
 
-def fold(results, fold_ref, block_ref, t0):
+def fold(results, fold_ref, block_ref, k, t0):
     for oy in range(3):
         sums = {}
         for g in range(2):
@@ -113,11 +113,11 @@
                         sums[kind] = sums[kind] + block if kind in sums else block
         p, u, q, s = sums[0, 0], sums[0, -2], sums[1, -1], sums[1, 1]
         first = lane(p.shape) < 64
-        block_ref[t0 + oy] = (q + turned(jnp.where(first, p, u))).astype(BF16)
+        block_ref[k, t0 + oy] = (q + turned(jnp.where(first, p, u))).astype(BF16)
         fold_ref[t0 + oy] = p + turned(s)
 
 
-def weight_sums(errors_t, source, count, pitch, fold_ref, block_ref, send):
+def weight_sums(errors_t, source, count, pitch, fold_ref, block_ref, k, send):
     def column(ox, carry):
         base = pl.multiple_of(ox * pitch, 16)
         results = []
@@ -129,9 +129,10 @@
             results.append(
                 jnp.dot(errors_t[g], window, preferred_element_type=F32)
             )
-        fold(results, fold_ref, block_ref, 3 * ox)
-        for oy in range(3):
-            send(3 * ox + oy)
+        fold(results, fold_ref, block_ref, k, 3 * ox)
+        if send:
+            for oy in range(3):
+                send(k, 3 * ox + oy)
         return carry
 
     lax.fori_loop(0, 3, column, 0)
@@ -139,16 +140,17 @@
     for i in range(5):
         even = turned(fold_ref[2 * i])
         odd = fold_ref[2 * i + 1] if i < 4 else jnp.zeros_like(even)
-        block_ref[9 + i] = jnp.where(first, even, odd).astype(BF16)
-        send(9 + i)
-
-
-def unfold(blocks_ref, per, out_ref, factor):
+        block_ref[k, 9 + i] = jnp.where(first, even, odd).astype(BF16)
+        if send:
+            send(k, 9 + i)
+
+
+def unfold(blocks_ref, per, k, out_ref, factor):
     for t in range(9):
-        block = blocks_ref[t // per, t % per].astype(F32) * factor
+        block = blocks_ref[k, t // per, t % per].astype(F32) * factor
         out_ref[192 * t : 192 * t + 128, :] = block.T
     for i in range(5):
-        block = (blocks_ref[(9 + i) // per, (9 + i) % per].astype(F32) * factor).T
+        block = (blocks_ref[k, (9 + i) // per, (9 + i) % per].astype(F32) * factor).T
         out_ref[384 * i + 128 : 384 * i + 192, :] = block[:64]
         if i < 4:
             out_ref[384 * i + 320 : 384 * i + 384, :] = block[64:]
@@ -278,6 +280,9 @@
         both = jnp.where(first, lows[:, x : x + 1], highs[:, x : x + 1]).astype(BF16)
         bounds[x] = both
         elh[x + 2, 16 : ny + 16, :] = both
+    def all_wait(like, sem):
+        pltpu.make_async_copy(like, like, sem).wait()
+
     def remote(src, dst, send, recv, to):
         return pltpu.make_async_remote_copy(
             src_ref=src,
@@ -293,24 +298,22 @@
 
     if comm:
         pl.semaphore_wait(barrier, len(peers))
-    halos = []
     if comm:
         x_from = {-1: slice(0, 2), 0: slice(0, nx), 1: slice(nx - 2, nx)}
         x_to = {-1: slice(nx + 2, nx + 4), 0: slice(2, nx + 2), 1: slice(0, 2)}
         y_from = {-1: slice(0, 16), 0: slice(0, ny), 1: slice(ny - 16, ny)}
         y_to = {-1: slice(ny + 16, ny + 32), 0: slice(16, ny + 16), 1: slice(0, 16)}
         order = sorted(HALOS, key=lambda h: -(2 * abs(h[0]) - abs(h[1])))
-        for i, (dx, dy) in enumerate(order):
+        for dx, dy in order:
             for k, (src, dst) in enumerate(((feat, ext), (bounds, elh))):
                 copy = remote(
                     src.at[x_from[dx], y_from[dy]],
                     dst.at[x_to[dx], y_to[dy]],
-                    halo_send.at[k, i],
-                    halo_recv.at[k, i],
+                    halo_send.at[k],
+                    halo_recv.at[k],
                     device(dx, dy),
                 )
                 copy.start()
-                halos.append(copy)
     inputs[1].wait()
     build_weights(w_two, fwd_two, adj_two)
     nothing = jnp.zeros((3, 2 * ROWS, WIDTH), BF16)
@@ -378,8 +381,10 @@
 
     own.wait()
     lax.fori_loop(0, nx // 2, mask_inner, 0, unroll=2)
-    for copy in halos:
-        copy.wait()
+    if comm:
+        margin = (nx + 4) * tall - nx * ny
+        for k, ref in enumerate((ext, elh)):
+            all_wait(ref.at[0 : margin // ny, 0:ny], halo_recv.at[k])
     if comm:
         for spot, inside in (
             ((slice(0, 2), slice(None)), gx > 0),
@@ -477,48 +482,24 @@
 
     lax.fori_loop(0, 8, spread, 0, unroll=2)
 
-    def block_copy(conv_id, b, sender):
-        return remote(
-            blocks.at[conv_id, b],
-            got_x.at[conv_id, sender, 0],
-            sum_send.at[conv_id, 0, b],
-            sum_recv.at[conv_id, 0, sender],
-            (b, gy),
-        )
-
-    def sender_of(conv_id):
-        def send(b):
-            if not comm:
-                got_x[conv_id, 0, b] = blocks[conv_id, b]
-                return
-
-            @pl.when(gx != b)
-            def _():
-                block_copy(conv_id, b, gx).start()
-
-            @pl.when(gx == b)
-            def _():
-                got_x[conv_id, gx, 0] = blocks[conv_id, b]
-
-        return send
-
-    def y_copy(conv_id, d):
-        return remote(
-            half.at[0, conv_id],
-            got_y.at[conv_id, gy],
-            sum_send.at[conv_id, 1, d],
-            sum_recv.at[conv_id, 1, d],
-            (gx, lax.rem(gy + d, n_gy)),
-        )
-
-    def full_copy(conv_id, to, owner):
-        return remote(
-            half.at[1, conv_id],
-            full.at[conv_id, owner],
-            sum_send.at[conv_id, 2, to],
-            sum_recv.at[conv_id, 2, owner],
-            (to, gy),
-        )
+    def send_block(k, b):
+        if not comm:
+            got_x[k, 0, b] = blocks[k, b]
+            return
+
+        @pl.when(gx != b)
+        def _():
+            remote(
+                blocks.at[k, b],
+                got_x.at[k, gx, 0],
+                sum_send.at[k, 0],
+                sum_recv.at[k, 0],
+                (b, gy),
+            ).start()
+
+        @pl.when(gx == b)
+        def _():
+            got_x[k, gx, 0] = blocks[k, b]
 
     def owners(act):
         if comm:
@@ -526,40 +507,48 @@
         else:
             act()
 
-    def others(n, act):
-        for k in range(n):
-            pl.when(gx != k)(functools.partial(act, k))
-
-    def reduce_x(conv_id):
+    def reduce_x(k):
         def act():
             if comm:
-                others(n_gx, lambda s: block_copy(conv_id, 0, s).wait_recv())
-            total = got_x[conv_id, 0].astype(F32)
+                all_wait(got_x.at[k, 0 : n_gx - 1], sum_recv.at[k, 0])
+            total = got_x[k, 0].astype(F32)
             for s in range(1, n_gx):
-                total = total + got_x[conv_id, s].astype(F32)
-            half[0, conv_id] = total.astype(BF16)
+                total = total + got_x[k, s].astype(F32)
+            half[0, k] = total.astype(BF16)
             for d in range(1, n_gy):
-                y_copy(conv_id, d).start()
-            got_y[conv_id, gy] = half[0, conv_id]
+                remote(
+                    half.at[0, k],
+                    got_y.at[k, gy],
+                    sum_send.at[k, 1],
+                    sum_recv.at[k, 1],
+                    (gx, lax.rem(gy + d, n_gy)),
+                ).start()
+            got_y[k, gy] = half[0, k]
 
         owners(act)
 
-    def reduce_y(conv_id):
+    def reduce_y(k):
         def act():
-            for d in range(1, n_gy):
-                y_copy(conv_id, d).wait_recv()
-            total = got_y[conv_id, 0].astype(F32)
+            if comm:
+                all_wait(got_y.at[k, 0 : n_gy - 1], sum_recv.at[k, 1])
+            total = got_y[k, 0].astype(F32)
             for s in range(1, n_gy):
-                total = total + got_y[conv_id, s].astype(F32)
-            half[1, conv_id] = total.astype(BF16)
-            if comm:
-                others(n_gx, lambda to: full_copy(conv_id, to, gx).start())
-            full[conv_id, gx] = half[1, conv_id]
+                total = total + got_y[k, s].astype(F32)
+            half[1, k] = total.astype(BF16)
+            for d in range(1, n_gx):
+                remote(
+                    half.at[1, k],
+                    full.at[k, gx],
+                    sum_send.at[k, 2],
+                    sum_recv.at[k, 2],
+                    (lax.rem(gx + d, n_gx), gy),
+                ).start()
+            full[k, gx] = half[1, k]
 
         owners(act)
 
     weight_sums(
-        errors_t, src_two, 8 * CORE, CORE, folded, blocks.at[1], sender_of(1)
+        errors_t, src_two, 8 * CORE, CORE, folded, blocks, 1, send_block
     )
 
     errors_t = []
@@ -574,7 +563,7 @@
             for oy, moved in enumerate(shifted(rows)):
                 err_one[oy, spot, lanes] = moved.astype(BF16)
     weight_sums(
-        errors_t, src_one, 10 * ROWS, ROWS, folded, blocks.at[0], sender_of(0)
+        errors_t, src_one, 10 * ROWS, ROWS, folded, blocks, 0, send_block
     )
     reduce_x(1)
 
@@ -637,6 +626,7 @@
     adjoint_one(0, [(2, 8)])
     reduce_x(0)
     adjoint_one(1, [(2, 8)])
+
     reduce_y(1)
 
     for x in range(2, nx + 2):
@@ -693,19 +683,24 @@
     lax.fori_loop(0, nx, finish, 0, unroll=4)
 
     if comm:
-        for conv_id in (1, 0):
-            others(USED, lambda k: full_copy(conv_id, 0, k).wait_recv())
         for copy in edges:
             copy.wait_send()
-        for conv_id in (1, 0):
-            others(USED, lambda b: block_copy(conv_id, b, gx).wait_send())
-
-            def sent(conv_id=conv_id):
-                for d in range(1, n_gy):
-                    y_copy(conv_id, d).wait_send()
-                others(n_gx, lambda to: full_copy(conv_id, to, gx).wait_send())
-
-            owners(sent)
+        for k, ref in enumerate((ext, elh)):
+            all_wait(ref.at[0 : margin // ny, 0:ny], halo_send.at[k])
+
+        @pl.when(gx < USED)
+        def _():
+            for k in range(2):
+                all_wait(full.at[k, 0 : USED - 1], sum_recv.at[k, 2])
+                all_wait(blocks.at[k, 0 : USED - 1], sum_send.at[k, 0])
+                all_wait(got_y.at[k, 0 : n_gy - 1], sum_send.at[k, 1])
+                all_wait(full.at[k, 0 : n_gx - 1], sum_send.at[k, 2])
+
+        @pl.when(gx >= USED)
+        def _():
+            for k in range(2):
+                all_wait(full.at[k, 0:USED], sum_recv.at[k, 2])
+                all_wait(blocks.at[k, 0:USED], sum_send.at[k, 0])
 
 
 def result_kernel(
@@ -718,7 +713,7 @@
     for copy in copies:
         copy.start()
     for k, (ref, gw) in enumerate(((one, gw_one), (two, gw_two))):
-        unfold(full.at[k], per, ref, factor)
+        unfold(full, per, k, ref, factor)
         copy = pltpu.make_async_copy(ref, gw, sem.at[2 + k])
         copy.start()
         copies.append(copy)
@@ -791,12 +786,12 @@
         vm((2, 2, 16, WIDTH), BF16),
         vm((2, 2, 16, WIDTH), BF16),
         dma((11,)),
-        dma((2, 8)),
-        dma((2, 8)),
+        dma((2,)),
+        dma((2,)),
         dma((8,)),
         dma((8,)),
-        dma((2, 3, 16)),
-        dma((2, 3, 16)),
+        dma((2, 3)),
+        dma((2, 3)),
     ]
     comm = n_gx * n_gy > 1
     params = pltpu.CompilerParams(

time: 51.2 us -> 50.5 us (0.986)
  Pallas kernels: 50.4 us -> 49.7 us
    pallas_call x1, Pallas kernels: 48.4 us -> 47.8 us  [run(): pl.pallas_call(functools.partial(block_kernel, n_gx, n_gy), out_shape=(co...]
where the time goes in v4:
time: 50.5 us; the launch traced here: 50.3 us
  Pallas kernels  49.7 us (98%)
  between operations  0.64 us (1%)
    pallas_call x1, Pallas kernels, run(): pl.pallas_call(functools.partial(block_kernel, n_gx, n_gy), out_shape=(co...  47.8 us
    pallas_call x1, Pallas kernels, run(): pl.pallas_call(functools.partial(result_kernel, 1.0 / (n_gx * n_gy * SHAR...  1.93 us

profile of v4, /device:TPU:1, one launch (start us, length us, event | category | flops | bytes accessed | tf_op | source)
XLA Modules:
  0.0 50.3 jit_solution(5426495792363750193)
XLA Ops:
  0.6 47.8 %residual_block.1 = (bf16[16,64,512]{2,1,0:T(8,128)(2,1)S(1)}, bf16[16,64,512]{2,1,0:T(8,128)(2,1)S(1)}, bf16[2,16,1,64,128]{4,3,2,1,0:T(8,128)(2,1)S(1)}) custom-call(bf16[16,64,512]{2,1,0:T(8,128)(2,1)} %feat.1, bf16[16,64,512]{2,1,0:T(8,128)(2,1)} %cot_in.1, bf16[1728,64]{1,0:T(8,128)(2,1)} %bitcast.8, bf16[1728,64]{1,0:T(8,128)(2,1)} %bitcast.9, ...), custom_call_target="tpu_custom_call" | custom-call | tf_op jit(solution)/shard_map/residual_block/pallas_call | solution.py:806
  48.4 1.9 %results.1 = (bf16[16,64,512]{2,1,0:T(8,128)(2,1)}, bf16[16,64,512]{2,1,0:T(8,128)(2,1)}, f32[1728,64]{1,0:T(8,128)}, f32[1728,64]{1,0:T(8,128)}) custom-call(bf16[16,64,512]{2,1,0:T(8,128)(2,1)S(1)} %get-tuple-element.11.out_in, bf16[16,64,512]{2,1,0:T(8,128)(2,1)S(1)} %get-tuple-element.12.gfeat_in, bf16[2,16,1,64,128]{4,3,2,1,0:T(8,128)(2,1)S(1)} %get-tuple-element.13.full), custom_call_target="tpu_custom_call" | custom-call | tf_op jit(solution)/shard_map/results/pallas_call | solution.py:831

commit v5 on v4

--- a/solution.py
+++ b/solution.py
@@ -68,7 +68,7 @@
         toeplitz(rows[64:192].T, rows[0:128].T, adjoint_ref, 8 - t)
         return carry
 
-    lax.fori_loop(0, 9, tap, 0)
+    lax.fori_loop(0, 9, tap, 0, unroll=3)
 
 
 def conv(source, band_ref, g, spans, pitch):
@@ -242,6 +242,10 @@
         return (lax.rem(gx + dx + n_gx, n_gx), lax.rem(gy + dy + n_gy, n_gy))
 
     if comm:
+        for ref in (ext, elh):
+            strip = jnp.zeros((nx + 4, 16, ref.shape[2]), BF16)
+            ref[:, 0:16, :] = strip
+            ref[:, ny + 16 : ny + 32, :] = strip
         barrier = pltpu.get_barrier_semaphore()
         peers = [(d, 0) for d in range(1, n_gx)] + [(0, d) for d in range(1, n_gy)]
         peers += [(dx, dy) for dx, dy in HALOS if dx and dy]
@@ -293,16 +297,18 @@
             device_id_type=MESH,
         )
 
-    inputs[0].wait()
-    build_weights(w_one, fwd_one, adj_one)
 
     if comm:
         pl.semaphore_wait(barrier, len(peers))
     if comm:
         x_from = {-1: slice(0, 2), 0: slice(0, nx), 1: slice(nx - 2, nx)}
         x_to = {-1: slice(nx + 2, nx + 4), 0: slice(2, nx + 2), 1: slice(0, 2)}
-        y_from = {-1: slice(0, 16), 0: slice(0, ny), 1: slice(ny - 16, ny)}
-        y_to = {-1: slice(ny + 16, ny + 32), 0: slice(16, ny + 16), 1: slice(0, 16)}
+        y_from = {-1: slice(0, 2), 0: slice(0, ny), 1: slice(ny - 2, ny)}
+        y_to = {
+            -1: slice(ny + 16, ny + 18),
+            0: slice(16, ny + 16),
+            1: slice(14, 16),
+        }
         order = sorted(HALOS, key=lambda h: -(2 * abs(h[0]) - abs(h[1])))
         for dx, dy in order:
             for k, (src, dst) in enumerate(((feat, ext), (bounds, elh))):
@@ -314,6 +320,8 @@
                     device(dx, dy),
                 )
                 copy.start()
+    inputs[0].wait()
+    build_weights(w_one, fwd_one, adj_one)
     inputs[1].wait()
     build_weights(w_two, fwd_two, adj_two)
     nothing = jnp.zeros((3, 2 * ROWS, WIDTH), BF16)
@@ -382,9 +390,9 @@
     own.wait()
     lax.fori_loop(0, nx // 2, mask_inner, 0, unroll=2)
     if comm:
-        margin = (nx + 4) * tall - nx * ny
+        margin = (nx + 4) * (ny + 4) - nx * ny
         for k, ref in enumerate((ext, elh)):
-            all_wait(ref.at[0 : margin // ny, 0:ny], halo_recv.at[k])
+            all_wait(ref.at[0 : margin // 48, 0:48], halo_recv.at[k])
     if comm:
         for spot, inside in (
             ((slice(0, 2), slice(None)), gx > 0),
@@ -686,7 +694,7 @@
         for copy in edges:
             copy.wait_send()
         for k, ref in enumerate((ext, elh)):
-            all_wait(ref.at[0 : margin // ny, 0:ny], halo_send.at[k])
+            all_wait(ref.at[0 : margin // 48, 0:48], halo_send.at[k])
 
         @pl.when(gx < USED)
         def _():

time: 50.5 us -> 48.7 us (0.964)
  Pallas kernels: 49.7 us -> 47.9 us
    pallas_call x1, Pallas kernels: 47.8 us -> 46 us  [run(): pl.pallas_call(functools.partial(block_kernel, n_gx, n_gy), out_shape=(co...]
where the time goes in v5:
time: 48.7 us; the launch traced here: 48.5 us
  Pallas kernels  47.9 us (98%)
  between operations  0.64 us (1%)
    pallas_call x1, Pallas kernels, run(): pl.pallas_call(functools.partial(block_kernel, n_gx, n_gy), out_shape=(co...  46 us
    pallas_call x1, Pallas kernels, run(): pl.pallas_call(functools.partial(result_kernel, 1.0 / (n_gx * n_gy * SHAR...  1.93 us

profile of v5, /device:TPU:1, one launch (start us, length us, event | category | flops | bytes accessed | tf_op | source)
XLA Modules:
  0.0 48.5 jit_solution(18208410978827350366)
XLA Ops:
  0.6 46.0 %residual_block.1 = (bf16[16,64,512]{2,1,0:T(8,128)(2,1)S(1)}, bf16[16,64,512]{2,1,0:T(8,128)(2,1)S(1)}, bf16[2,16,1,64,128]{4,3,2,1,0:T(8,128)(2,1)S(1)}) custom-call(bf16[16,64,512]{2,1,0:T(8,128)(2,1)} %feat.1, bf16[16,64,512]{2,1,0:T(8,128)(2,1)} %cot_in.1, bf16[1728,64]{1,0:T(8,128)(2,1)} %bitcast.8, bf16[1728,64]{1,0:T(8,128)(2,1)} %bitcast.9, ...), custom_call_target="tpu_custom_call" | custom-call | tf_op jit(solution)/shard_map/residual_block/pallas_call | solution.py:814
  46.6 1.9 %results.1 = (bf16[16,64,512]{2,1,0:T(8,128)(2,1)}, bf16[16,64,512]{2,1,0:T(8,128)(2,1)}, f32[1728,64]{1,0:T(8,128)}, f32[1728,64]{1,0:T(8,128)}) custom-call(bf16[16,64,512]{2,1,0:T(8,128)(2,1)S(1)} %get-tuple-element.11.out_in, bf16[16,64,512]{2,1,0:T(8,128)(2,1)S(1)} %get-tuple-element.12.gfeat_in, bf16[2,16,1,64,128]{4,3,2,1,0:T(8,128)(2,1)S(1)} %get-tuple-element.13.full), custom_call_target="tpu_custom_call" | custom-call | tf_op jit(solution)/shard_map/results/pallas_call | solution.py:839

commit v6 on v5

--- a/solution.py
+++ b/solution.py
@@ -118,8 +118,8 @@
 
 
 def weight_sums(errors_t, source, count, pitch, fold_ref, block_ref, k, send):
-    def column(ox, carry):
-        base = pl.multiple_of(ox * pitch, 16)
+    for ox in range(3):
+        base = ox * pitch
         results = []
         for g in range(2):
             lanes = slice(128 * g, 128 * g + 384)
@@ -133,9 +133,6 @@
         if send:
             for oy in range(3):
                 send(k, 3 * ox + oy)
-        return carry
-
-    lax.fori_loop(0, 3, column, 0)
     first = lane((64, 128)) < 64
     for i in range(5):
         even = turned(fold_ref[2 * i])
@@ -439,7 +436,7 @@
             core_mask[pl.ds(core, CORE), lanes] = value[ROWS:]
         return carry
 
-    lax.fori_loop(0, W, cut, 0, unroll=4)
+    lax.fori_loop(0, W, cut, 0, unroll=12)
 
     scale_one, shift_one, scale_two, shift_two = (
         jnp.concatenate([scales[k]] * 4, axis=1) for k in range(4)

time: 48.7 us -> 47.7 us (0.979)
  Pallas kernels: 47.9 us -> 46.8 us
    pallas_call x1, Pallas kernels: 46 us -> 44.8 us  [run(): pl.pallas_call(functools.partial(block_kernel, n_gx, n_gy), out_shape=(co...]
where the time goes in v6:
time: 47.7 us; the launch traced here: 47.6 us
  Pallas kernels  46.8 us (98%)
  between operations  0.8 us (2%)
    pallas_call x1, Pallas kernels, run(): pl.pallas_call(functools.partial(block_kernel, n_gx, n_gy), out_shape=(co...  44.8 us
    pallas_call x1, Pallas kernels, run(): pl.pallas_call(functools.partial(result_kernel, 1.0 / (n_gx * n_gy * SHAR...  1.93 us

profile of v6, /device:TPU:1, one launch (start us, length us, event | category | flops | bytes accessed | tf_op | source)
XLA Modules:
  0.0 47.6 jit_solution(1386465672837273737)
XLA Ops:
  0.6 44.8 %residual_block.1 = (bf16[16,64,512]{2,1,0:T(8,128)(2,1)S(1)}, bf16[16,64,512]{2,1,0:T(8,128)(2,1)S(1)}, bf16[2,16,1,64,128]{4,3,2,1,0:T(8,128)(2,1)S(1)}) custom-call(bf16[16,64,512]{2,1,0:T(8,128)(2,1)} %feat.1, bf16[16,64,512]{2,1,0:T(8,128)(2,1)} %cot_in.1, bf16[1728,64]{1,0:T(8,128)(2,1)} %bitcast.8, bf16[1728,64]{1,0:T(8,128)(2,1)} %bitcast.9, ...), custom_call_target="tpu_custom_call" | custom-call | tf_op jit(solution)/shard_map/residual_block/pallas_call | solution.py:811
  45.5 1.9 %results.1 = (bf16[16,64,512]{2,1,0:T(8,128)(2,1)}, bf16[16,64,512]{2,1,0:T(8,128)(2,1)}, f32[1728,64]{1,0:T(8,128)}, f32[1728,64]{1,0:T(8,128)}) custom-call(bf16[16,64,512]{2,1,0:T(8,128)(2,1)S(1)} %get-tuple-element.11.out_in, bf16[16,64,512]{2,1,0:T(8,128)(2,1)S(1)} %get-tuple-element.12.gfeat_in, bf16[2,16,1,64,128]{4,3,2,1,0:T(8,128)(2,1)S(1)} %get-tuple-element.13.full), custom_call_target="tpu_custom_call" | custom-call | tf_op jit(solution)/shard_map/results/pallas_call | solution.py:836

commit v7 on v6

--- a/solution.py
+++ b/solution.py
@@ -485,7 +485,7 @@
                 err_two[oy, pl.ds(base, ROWS), lanes] = moved.astype(BF16)
         return carry
 
-    lax.fori_loop(0, 8, spread, 0, unroll=2)
+    lax.fori_loop(0, 8, spread, 0, unroll=8)
 
     def send_block(k, b):
         if not comm:
@@ -653,7 +653,7 @@
         out[8 + x] = value[ny:]
         return carry
 
-    lax.fori_loop(0, 8, deposit, 0, unroll=4)
+    lax.fori_loop(0, 8, deposit, 0, unroll=8)
 
     if comm:
         for copy in edges:

time: 47.7 us -> 47.7 us (level)
  no operation moved by 1% of the time
where the time goes in v7:
time: 47.7 us; the launch traced here: 47.5 us
  Pallas kernels  46.7 us (98%)
  between operations  0.8 us (2%)
    pallas_call x1, Pallas kernels, run(): pl.pallas_call(functools.partial(block_kernel, n_gx, n_gy), out_shape=(co...  44.8 us
    pallas_call x1, Pallas kernels, run(): pl.pallas_call(functools.partial(result_kernel, 1.0 / (n_gx * n_gy * SHAR...  1.93 us

profile of v7, /device:TPU:1, one launch (start us, length us, event | category | flops | bytes accessed | tf_op | source)
XLA Modules:
  0.0 47.5 jit_solution(5645211229463219013)
XLA Ops:
  0.6 44.8 %residual_block.1 = (bf16[16,64,512]{2,1,0:T(8,128)(2,1)S(1)}, bf16[16,64,512]{2,1,0:T(8,128)(2,1)S(1)}, bf16[2,16,1,64,128]{4,3,2,1,0:T(8,128)(2,1)S(1)}) custom-call(bf16[16,64,512]{2,1,0:T(8,128)(2,1)} %feat.1, bf16[16,64,512]{2,1,0:T(8,128)(2,1)} %cot_in.1, bf16[1728,64]{1,0:T(8,128)(2,1)} %bitcast.8, bf16[1728,64]{1,0:T(8,128)(2,1)} %bitcast.9, ...), custom_call_target="tpu_custom_call" | custom-call | tf_op jit(solution)/shard_map/residual_block/pallas_call | solution.py:811
  45.4 1.9 %results.1 = (bf16[16,64,512]{2,1,0:T(8,128)(2,1)}, bf16[16,64,512]{2,1,0:T(8,128)(2,1)}, f32[1728,64]{1,0:T(8,128)}, f32[1728,64]{1,0:T(8,128)}) custom-call(bf16[16,64,512]{2,1,0:T(8,128)(2,1)S(1)} %get-tuple-element.11.out_in, bf16[16,64,512]{2,1,0:T(8,128)(2,1)S(1)} %get-tuple-element.12.gfeat_in, bf16[2,16,1,64,128]{4,3,2,1,0:T(8,128)(2,1)S(1)} %get-tuple-element.13.full), custom_call_target="tpu_custom_call" | custom-call | tf_op jit(solution)/shard_map/results/pallas_call | solution.py:836
